TPU v7x, 32 devices: a whole 2x2x4 slice. The times are simulated.
32 devices in a mesh: sub: 16 (over z, y, x), grp: 2 (over core).
Axes of the slice: x: 2, y: 2, z: 4, core: 2. Of those that a mesh axis runs over, the one named last changes fastest.
Arguments:
- interior_factor: bfloat16 [16, 1024, 1024], P('sub'), may hold values from -2 to 2, as said below
- coupling: bfloat16 [16, 512, 1024], P('sub', 'grp'), may hold values from -0.09375 to 0.09375
- boundary_stiffness: float32 [16, 512, 512], P('sub', 'grp'), may hold values from -0.65625 to 9, as said below
- interior_mass: float32 [16, 1024], P('sub'), may hold values from 0.5 to 4
- boundary_mass: float32 [16, 512], P('sub', 'grp'), may hold values from 0.5 to 2
- dof_map: int32 [16, 256], P('sub'), may hold values from 0 to 255, each once within a row
- load_cases: float32 [16, 64, 256], P('sub'), may hold values from -30 to 30
Outputs:
- reduced_stiffness: float32 [16, 256, 256], P('sub')
- reduced_mass: float32 [16, 256, 256], P('sub')
- displacement: float32 [16, 64, 256], P('sub')
Inputs may be any that keep to these rules, and one draw needn't show every extreme that they name: `interior_factor`: lower triangular; diagonal between 1 and 2. `boundary_stiffness`: symmetric; diagonal between 6 and 9. `dof_map`: each row a permutation of 0 to 255.
All inputs are finite; a program needn't handle non-finite values.
Results may differ from a plain program's by a relative error of at most 0.00095.
Values may be sent and summed in bfloat16 or wider, within the bound.
A program may use at most 64 MiB of HBM per device.

v0:
```python
import jax
import jax.numpy as jnp
from jax import lax
from jax.sharding import PartitionSpec as P

ITERS = 2


HIGH = lax.Precision.HIGHEST


def passed_along(array, axis, by):
    size = lax.axis_size(axis)
    return lax.ppermute(array, axis, [(i, (i + by) % size) for i in range(size)])


def inner_block(left, right):
    return lax.dot_general(left, right, (((1,), (1,)), ((), ())), precision=HIGH)


def chol_solve(matrix, right):
    return jax.scipy.linalg.cho_solve((jnp.linalg.cholesky(matrix), True), right)


def shards(
    interior_factor, coupling, boundary_stiffness, interior_mass, boundary_mass, dof_map, load_cases
):
    factor = interior_factor[0].astype(jnp.float32)
    stiff_rows = boundary_stiffness[0]
    width = stiff_rows.shape[0]
    nbound = stiff_rows.shape[1]
    half = nbound // 2
    offset = lax.axis_index("grp") * width
    weights = interior_mass[0]
    modes_own = jax.scipy.linalg.solve_triangular(
        factor, coupling[0].astype(jnp.float32).T, lower=True
    )
    constraint_own = -jax.scipy.linalg.solve_triangular(factor, modes_own, lower=True, trans=1)
    modes_rows = modes_own.T
    constraint_rows = constraint_own.T
    weighted_rows = (weights[:, None] * constraint_own).T
    empty = jnp.zeros((width, nbound), jnp.float32)
    carry = (empty, empty)
    start = jnp.int32(0)
    stiff_part = carry[0] + inner_block(
        modes_rows,
        lax.all_gather(modes_rows.astype(jnp.bfloat16), "grp", axis=0, tiled=True).astype(
            jnp.float32
        ),
    )
    mass_part = carry[1] + inner_block(
        weighted_rows,
        lax.all_gather(constraint_rows.astype(jnp.bfloat16), "grp", axis=0, tiled=True).astype(
            jnp.float32
        ),
    )
    cross_stiff = lax.dynamic_update_slice_in_dim(carry[0], stiff_part, start, 1)
    cross_mass = lax.dynamic_update_slice_in_dim(carry[1], mass_part, start, 1)
    schur_rows = stiff_rows - cross_stiff
    columns = lax.broadcasted_iota(jnp.int32, (width, nbound), 1)
    row_numbers = lax.broadcasted_iota(jnp.int32, (width, nbound), 0) + offset
    mass_rows = cross_mass + jnp.where(columns == row_numbers, boundary_mass[0][:, None], 0.0)
    start_col = offset // half * half
    stiff_piece = lax.dynamic_slice_in_dim(schur_rows, start_col, half, 1)
    mass_piece = lax.dynamic_slice_in_dim(mass_rows, start_col, half, 1)
    mapping = dof_map[0]
    inverse = jnp.zeros((half,), jnp.int32).at[mapping].set(jnp.arange(half, dtype=jnp.int32))
    stiff_faces, mass_faces = (
        lax.all_gather(stiff_piece, "grp", axis=0, tiled=True),
        lax.all_gather(mass_piece, "grp", axis=0, tiled=True),
    )
    shared_stiff = stiff_faces[half:][inverse][:, inverse]
    shared_mass = mass_faces[half:][inverse][:, inverse]
    came_stiff, came_mass = passed_along((shared_stiff, shared_mass), "sub", -1)
    reduced_stiff = stiff_faces[:half] + came_stiff
    reduced_masses = mass_faces[:half] + came_mass
    lower_factor = jnp.linalg.cholesky(reduced_stiff)

    def precondition(values):
        return jax.scipy.linalg.cho_solve((lower_factor, True), values.T).T

    residual = load_cases[0]
    solution = jnp.zeros_like(residual)
    smoothed = precondition(residual)
    rho_sum = lax.psum(inner_block(residual, smoothed), "sub")
    direction = smoothed
    for step in range(ITERS):
        previous = passed_along(direction, "sub", 1)
        local_dirs = jnp.concatenate([direction, jnp.take(previous, mapping, axis=1)], axis=1)
        piece = inner_block(local_dirs, schur_rows)
        images = lax.all_gather(piece, "grp", axis=1, tiled=True)
        shared = jnp.take(images[:, half:], inverse, axis=1)
        returned = passed_along(shared, "sub", -1)
        images = images[:, :half] + returned
        smoothed_images = precondition(images)
        gamma_sum, cross_sum, curve_sum = lax.psum(
            (
                inner_block(direction, images),
                inner_block(residual, smoothed_images),
                inner_block(images, smoothed_images),
            ),
            "sub",
        )
        step_coeffs = chol_solve(gamma_sum, rho_sum)
        solution = solution + jnp.dot(step_coeffs.T, direction, precision=HIGH)
        residual = residual - jnp.dot(step_coeffs.T, images, precision=HIGH)
        if step + 1 < ITERS:
            cross_term = jnp.dot(cross_sum, step_coeffs, precision=HIGH)
            rho_next = (
                rho_sum
                - cross_term
                - cross_term.T
                + jnp.dot(
                    step_coeffs.T, jnp.dot(curve_sum, step_coeffs, precision=HIGH), precision=HIGH
                )
            )
            smoothed = smoothed - jnp.dot(step_coeffs.T, smoothed_images, precision=HIGH)
            next_coeffs = chol_solve(rho_sum, rho_next)
            direction = smoothed + jnp.dot(next_coeffs.T, direction, precision=HIGH)
            rho_sum = rho_next
    return (reduced_stiff[None], reduced_masses[None], solution[None])


def solution(mesh):
    return jax.shard_map(
        shards,
        mesh=mesh,
        in_specs=(
            P("sub", None, None),
            P("sub", "grp", None),
            P("sub", "grp", None),
            P("sub", None),
            P("sub", "grp"),
            P("sub", None),
            P("sub", None, None),
        ),
        out_specs=(P("sub", None, None), P("sub", None, None), P("sub", None, None)),
        check_vma=False,
    )
```

profile of v0, /device:TPU:0, one launch (start us, length us, event | category | flops | bytes accessed | tf_op | source)
XLA Modules:
  0.0 504.8 jit_solution(5306574552333152351)
XLA Ops:
  7.2 4.1 convert_select_fusion
  11.3 22.5 %while.5 = (s32[]{:T(128)}, f32[1024,1024]{1,0:T(8,128)}, s32[8,2]{0,1:T(2,128)S(1)}, f32[8,128,128]{2,1,0:T(8,128)S(1)}, s32[]{:T(128)}) while((s32[]{:T(128)}, f32[1024,1024]{1,0:T(8,128)}, s32[8,2]{0,1:T(2,128)S(1)}, f32[8,128,128]{2,1,0:T(8,128)S(1)}, s32[]{:T(128)}) %tuple.80), condition=%wide.while_cond.1, body=%wide.while_body.1.sunk | while | flops 2 | bytes 131181 | solution.py:35
  33.8 78.6 %custom-call.30 = f32[8,128,128]{1,2,0:T(8,128)S(1)} custom-call(f32[8,128,128]{2,1,0:T(8,128)S(1)} %get-tuple-element.22), custom_call_target="InvertDiagBlocksLowerTriangular" | custom-call | tf_op jit(solution)/shard_map/jit(_solve_triangular)/triangular_solve | solution.py:35
  125.9 2.7 convolution_subtract_fusion.14
  155.3 7.4 %collective-permute-start = (f32[256,256]{0,1:T(8,128)}, f32[256,256]{0,1:T(8,128)S(1)}, u32[]{:S(2)}, u32[]{:S(2)}) collective-permute-start(f32[256,256]{0,1:T(8,128)} %bitcast.16), channel_id=1, source_target_pairs={{0,30},{2,0},{4,2},{6,4},{8,6},{10,8},{12,10},{14,12},{16,14},{18,... | collective-permute-start | bytes 786440 | tf_op jit(solution)/shard_map/ppermute | solution.py:14
  162.7 2.6 fusion.1
  165.3 3.6 collective-permute-done
  169.1 11.7 %cholesky.64 = f32[128,128]{1,0:T(8,128)S(1)} custom-call(f32[128,128]{1,0:T(8,128)S(1)} %cholesky.208), custom_call_target="Cholesky" | custom-call | tf_op jit(solution)/shard_map/jit(cholesky)/cholesky | solution.py:77
  180.9 9.8 %custom-call.31 = f32[1,128,128]{1,2,0:T(8,128)S(1)} custom-call(f32[1,128,128]{2,1,0:T(8,128)S(1)} %get-tuple-element.89), custom_call_target="InvertDiagBlocksLowerTriangular" | custom-call | tf_op jit(solution)/shard_map/jit(cholesky)/cholesky | solution.py:77
  191.2 11.7 %cholesky.132 = f32[128,128]{1,0:T(8,128)S(1)} custom-call(f32[128,128]{1,0:T(8,128)S(1)} %slice_subtract_fusion), custom_call_target="Cholesky" | custom-call | tf_op jit(solution)/shard_map/jit(cholesky)/cholesky | solution.py:77
  204.9 5.3 %while.6 = (s32[]{:T(128)}, f32[256,256]{1,0:T(8,128)S(1)}, s32[2,2]{1,0:T(2,128)S(1)}, f32[2,128,128]{2,1,0:T(8,128)}, s32[]{:T(128)}) while((s32[]{:T(128)}, f32[256,256]{1,0:T(8,128)S(1)}, s32[2,2]{1,0:T(2,128)S(1)}, f32[2,128,128]{2,1,0:T(8,128)}, s32[]{:T(128)}) %tuple.83), condition=%wide.while_cond, body=%wide.while_body.sunk | while | flops 2 | bytes 132705 | solution.py:80
  210.3 20.5 %custom-call.35 = f32[2,128,128]{1,2,0:T(8,128)S(1)} custom-call(f32[2,128,128]{2,1,0:T(8,128)} %get-tuple-element.29), custom_call_target="InvertDiagBlocksLowerTriangular" | custom-call | tf_op jit(solution)/shard_map/jit(_cho_solve)/triangular_solve | solution.py:80
  232.4 8.1 %collective-permute-done.2 = f32[64,256]{1,0:T(8,128)S(1)} collective-permute-done((f32[64,256]{1,0:T(8,128)S(1)}, f32[64,256]{1,0:T(8,128)S(1)}, u32[]{:S(2)}, u32[]{:S(2)}) %collective-permute-start.2) | collective-permute-done | bytes 65568 | tf_op jit(solution)/shard_map/ppermute | solution.py:14
  257.3 5.7 %collective-permute-start.1 = (f32[256,256]{1,0:T(8,128)S(1)}, f32[256,256]{1,0:T(8,128)S(1)}, u32[]{:S(2)}, u32[]{:S(2)}) collective-permute-start(f32[256,256]{1,0:T(8,128)S(1)} %bitcast.251), channel_id=1, source_target_pairs={{0,30},{2,0},{4,2},{6,4},{8,6},{10,8},{12,10},{14,12},{16,14},{18,... | collective-permute-start | bytes 786440 | tf_op jit(solution)/shard_map/ppermute | solution.py:14
  263.0 96.9 %all-reduce.4.cloned.1.call-done = (f32[64,64]{0,1:T(8,128)}, f32[64,64]{0,1:T(8,128)}, f32[64,64]{1,0:T(8,128)}, f32[64,64]{0,1:T(8,128)}) async-done(((f32[64,64]{0,1:T(8,128)}, f32[64,64]{0,1:T(8,128)}, f32[64,64]{1,0:T(8,128)}, f32[64,64]{0,1:T(8,128)}), (f32[64,64]{0,1:T(8,128)}, f32[64,64]{0,1:T(8,128)}, f32[64,64]{1,0:T(8,128)}, f32[64,64]{0,1:T(8,128)})) %all-reduce.4.cloned.1.call-update) | async-done | bytes 65552 | tf_op jit(solution)/shard_map/psum | solution.py:85
  361.5 5.8 %cholesky.188 = f32[64,64]{1,0:T(8,128)S(1)} custom-call(f32[64,64]{1,0:T(8,128)S(1)} %fusion.110), custom_call_target="Cholesky" | custom-call | tf_op jit(solution)/shard_map/jit(cholesky)/cholesky | solution.py:22
  368.6 4.9 custom-call.38
  375.2 5.8 %cholesky.177 = f32[64,64]{1,0:T(8,128)S(1)} custom-call(f32[64,64]{1,0:T(8,128)S(1)} %fusion.115), custom_call_target="Cholesky" | custom-call | tf_op jit(solution)/shard_map/jit(cholesky)/cholesky | solution.py:22
  382.4 4.9 custom-call.36
  395.5 4.8 collective-permute-done.4
  405.0 4.0 collective-permute-done.5
  409.2 75.4 %psum.39 = f32[64,64]{0,1:T(8,128)S(1)} all-reduce(f32[64,64]{0,1:T(8,128)S(1)} %fusion.58), channel_id=1, replica_groups=mesh['sub'=16,'grp'=2] {'sub'}, use_global_device_ids=true, to_apply=%region_11.16 | all-reduce | flops 4096 | bytes 32768 | tf_op jit(solution)/shard_map/psum | solution.py:96
  484.7 5.8 %cholesky.199 = f32[64,64]{1,0:T(8,128)S(1)} custom-call(f32[64,64]{1,0:T(8,128)S(1)} %fusion.105), custom_call_target="Cholesky" | custom-call | tf_op jit(solution)/shard_map/jit(cholesky)/cholesky | solution.py:22
  491.8 4.9 custom-call.39
  (223 shorter events, 108.5 us)
Async XLA Ops:
  7.2 105.3 %copy-start = (bf16[1,256,1024]{2,1,0:T(8,128)(2,1)S(1)}, bf16[1,256,1024]{2,1,0:T(8,128)(2,1)}, u32[]{:S(2)}) copy-start(bf16[1,256,1024]{2,1,0:T(8,128)(2,1)} %param.15) | copy-start | bytes 1572868
  7.2 140.4 %all-gather.3.cloned.1.call-start = ((), (), s32[]{:S(2)}) async-start(), calls=%async_computation | async-start | bytes 1572864 | tf_op jit(solution)/shard_map/all_gather | solution.py:47
  129.8 32.9 %all-gather.5.cloned.1.call-start = ((), (), s32[]{:S(2)}) async-start(), calls=%async_computation.1 | async-start | bytes 1572864 | tf_op jit(solution)/shard_map/all_gather | solution.py:53
  140.9 3.8 copy-start.3
  144.6 215.2 %all-reduce.4.cloned.1.call-start = ((), (), s32[]{:S(2)}) async-start(), calls=%async_computation.2 | async-start | bytes 262144 | tf_op jit(solution)/shard_map/psum | solution.py:85
  150.1 12.6 %copy-start.2 = (f32[1,1024]{1,0:T(1,128)S(1)}, f32[1,1024]{1,0:T(1,128)}, u32[]{:S(2)}) copy-start(f32[1,1024]{1,0:T(1,128)} %param.17) | copy-start | bytes 12292
  155.3 75.4 %copy-start.1 = (f32[1,64,256]{2,1,0:T(8,128)S(1)}, f32[1,64,256]{2,1,0:T(8,128)}, u32[]{:S(2)}) copy-start(f32[1,64,256]{2,1,0:T(8,128)} %param.20) | copy-start | bytes 196612
  155.3 13.5 %collective-permute-start = (f32[256,256]{0,1:T(8,128)}, f32[256,256]{0,1:T(8,128)S(1)}, u32[]{:S(2)}, u32[]{:S(2)}) collective-permute-start(f32[256,256]{0,1:T(8,128)} %bitcast.16), channel_id=1, source_target_pairs={{0,30},{2,0},{4,2},{6,4},{8,6},{10,8},{12,10},{14,12},{16,14},{18,... | collective-permute-start | bytes 786440 | tf_op jit(solution)/shard_map/ppermute | solution.py:14
  162.7 69.6 %copy-start.4 = (f32[1,256]{1,0:T(1,128)S(1)}, f32[1,256]{1,0:T(1,128)}, u32[]{:S(2)}) copy-start(f32[1,256]{1,0:T(1,128)} %param.18) | copy-start | bytes 3076
  232.2 8.3 %collective-permute-start.2 = (f32[64,256]{1,0:T(8,128)S(1)}, f32[64,256]{1,0:T(8,128)S(1)}, u32[]{:S(2)}, u32[]{:S(2)}) collective-permute-start(f32[64,256]{1,0:T(8,128)S(1)} %fusion.118), channel_id=1, source_target_pairs={{0,2},{2,4},{4,6},{6,8},{8,10},{10,12},{12,14},{14,16},{16,18},{18... | collective-permute-start | bytes 196616 | tf_op jit(solution)/shard_map/ppermute | solution.py:14
  244.6 4.3 collective-permute-start.3
  257.3 136.6 %collective-permute-start.1 = (f32[256,256]{1,0:T(8,128)S(1)}, f32[256,256]{1,0:T(8,128)S(1)}, u32[]{:S(2)}, u32[]{:S(2)}) collective-permute-start(f32[256,256]{1,0:T(8,128)S(1)} %bitcast.251), channel_id=1, source_target_pairs={{0,30},{2,0},{4,2},{6,4},{8,6},{10,8},{12,10},{14,12},{16,14},{18,... | collective-permute-start | bytes 786440 | tf_op jit(solution)/shard_map/ppermute | solution.py:14
  392.4 7.9 %collective-permute-start.4 = (f32[64,256]{1,0:T(8,128)S(1)}, f32[64,256]{1,0:T(8,128)S(1)}, u32[]{:S(2)}, u32[]{:S(2)}) collective-permute-start(f32[64,256]{1,0:T(8,128)S(1)} %convolution_add_fusion.1), channel_id=1, source_target_pairs={{0,2},{2,4},{4,6},{6,8},{8,10},{10,12},{12,14},{14,16},{16,18},{18... | collective-permute-start | bytes 196616 | tf_op jit(solution)/shard_map/ppermute | solution.py:14
  404.7 4.3 collective-permute-start.5
Sparse Core Ops, SparseCore 0:
  129.9 11.6 all-gather.2
  144.8 11.6 all-gather.4
  253.0 106.7 all-reduce.3
where the time goes:
time: 514 us; the launch traced here: 505 us
  other arithmetic  178 us (35%)
  waiting for transfers between devices  119 us (23%)
  blocking collectives  83.8 us (16%)
  matrix products  48.4 us (9%)
  local copies, waits for them, and re-layouts  42.1 us (8%)
  starting transfers between devices  17.2 us (3%)
  between operations  16.4 us (3%)
    psum x1, waiting for transfers between devices, shards(): rho_sum = lax.psum(inner_block(residual, smoothed), 'sub')  96.9 us
    another operation x3, other arithmetic, shards(): jax.scipy.linalg.solve_triangular(factor, coupling[0].astype(jnp.float32)...  82.7 us
    psum x1, blocking collectives, shards(): lax.psum((inner_block(direction, images), inner_block(residual, smoothed_...  75.4 us
    another operation x6, other arithmetic, shards(): lower_factor = jnp.linalg.cholesky(reduced_stiff)  34 us
    another operation x24, local copies, waits for them, and re-layouts  22.3 us
    ppermute x6, waiting for transfers between devices, passed_along(): lax.ppermute(array, axis, [(i, (i + by) % size) for i in range(size)])  21.9 us
    another operation x4, other arithmetic, precondition(): return jax.scipy.linalg.cho_solve((lower_factor, True), values.T).T  20.5 us
    another operation x9, other arithmetic, chol_solve(): jnp.linalg.cholesky(matrix)  19.6 us
  transfers between devices with their start and end apart: 9, of which 6 were waited for; matrix products, arithmetic and copies ran while one was open for 12% of the time, Pallas kernels for 0%

commit v1 on v0

v1 whole, which is shorter than its diff:
```python
import functools
import jax
import jax.numpy as jnp
from jax import lax
from jax.experimental import pallas as pl
from jax.experimental.pallas import tpu as pltpu
from jax.sharding import PartitionSpec as P

F32 = jnp.float32
BF16 = jnp.bfloat16
HIGH = lax.Precision.HIGHEST
TILE = 128
VMEM_LIMIT = 48 * 2**20
NT = (((1,), (1,)), ((), ()))
NN = (((1,), (0,)), ((), ()))
TN = (((0,), (0,)), ((), ()))


def dot(a, b, dims=NN):
    return lax.dot_general(a, b, dims, preferred_element_type=F32)


def fdot(a, b, dims=NN):
    return lax.dot_general(a, b, dims, precision=HIGH, preferred_element_type=F32)


def split(x):
    hi = x.astype(BF16)
    return hi, (x - hi.astype(F32)).astype(BF16)


def dot3(a, b, dims=NN):
    ah, al = split(a)
    bh, bl = split(b)
    return dot(ah, bh, dims) + (dot(ah, bl, dims) + dot(al, bh, dims))


def iota(shape, dim):
    return lax.broadcasted_iota(jnp.int32, shape, dim)


def modes_kernel(l_ref, c_ref, w_ref, k_ref, inv, wh, wl):
    ni = l_ref.shape[0]
    count = ni // TILE
    rows = iota((TILE, TILE), 0)
    cols = iota((TILE, TILE), 1)

    def block(j):
        return l_ref[j * TILE : (j + 1) * TILE, j * TILE : (j + 1) * TILE]

    pair = ((rows >> 1) == (cols >> 1)) & (rows > cols)
    for j in range(count):
        full = block(j).astype(F32)
        diag = jnp.where(rows == cols, full, 0.0)
        down = 1.0 / jnp.sum(diag, axis=1, keepdims=True)
        across = 1.0 / jnp.sum(diag, axis=0, keepdims=True)
        first = jnp.where(rows == cols, down, 0.0)
        inv[j] = first - jnp.where(pair, down * full * across, 0.0)

    levels = TILE.bit_length() - 1

    def level(lev, carry):
        same = (rows >> (lev + 1)) == (cols >> (lev + 1))
        low = ((rows >> lev) & 1) > ((cols >> lev) & 1)
        mask = same & low
        for j in range(count):
            x = inv[j]
            off = jnp.where(mask, block(j).astype(F32), 0.0).astype(BF16)
            xh, xl = split(x)
            mid = dot(xh, off) + dot(xl, off)
            mh, ml = split(mid)
            inv[j] = x - (dot(mh, xh) + (dot(mh, xl) + dot(ml, xh)))
        return carry

    lax.fori_loop(1, levels, level, 0)

    for j in range(count):
        at = slice(j * TILE, (j + 1) * TILE)
        acc = c_ref[:, at].astype(F32)
        if j:
            before = slice(0, j * TILE)
            acc = acc - (
                dot(wh[:, before], l_ref[at, before], NT)
                + dot(wl[:, before], l_ref[at, before], NT)
            )
        piece = dot3(acc, inv[j], NT)
        hi, lo = split(piece)
        wh[:, at] = hi
        wl[:, at] = lo
        w_ref[:, at] = hi
    for j in reversed(range(count)):
        at = slice(j * TILE, (j + 1) * TILE)
        acc = wh[:, at].astype(F32) + wl[:, at].astype(F32)
        if j + 1 < count:
            after = slice((j + 1) * TILE, ni)
            acc = acc + (dot(wh[:, after], l_ref[after, at]) + dot(wl[:, after], l_ref[after, at]))
        piece = -dot3(acc, inv[j])
        hi, lo = split(piece)
        wh[:, at] = hi
        wl[:, at] = lo
        k_ref[:, at] = hi


def modes(factor, coupling):
    width, ni = coupling.shape
    return pl.pallas_call(
        modes_kernel,
        out_shape=[jax.ShapeDtypeStruct((width, ni), BF16)] * 2,
        scratch_shapes=[
            pltpu.VMEM((ni // TILE, TILE, TILE), F32),
            pltpu.VMEM((width, ni), BF16),
            pltpu.VMEM((width, ni), BF16),
        ],
        compiler_params=pltpu.CompilerParams(vmem_limit_bytes=VMEM_LIMIT),
        name="modes",
    )(factor, coupling)


def faces_kernel(w_ref, k_ref, stiff_ref, mass_ref, bound_ref, map_ref, own_ref, move_ref, om_ref, mm_ref):
    half = stiff_ref.shape[0] // 2
    wo, ws = w_ref[:half], w_ref[half:]
    own_ref[...] = stiff_ref[:half, :half] - dot(wo, wo, NT)
    shared = stiff_ref[half:, half:] - dot(ws, ws, NT)
    cross = stiff_ref[half:, :half] - dot(ws, wo, NT)
    weights = mass_ref[...]
    eye = iota((half, half), 0) == iota((half, half), 1)

    def mass_of(c, b):
        ch, cl = split(c.astype(F32) * weights)
        return dot(ch, c, NT) + dot(cl, c, NT) + jnp.where(eye, b, 0.0)

    om_ref[...] = mass_of(k_ref[:half], bound_ref[:, :half])
    mass_shared = mass_of(k_ref[half:], bound_ref[:, half:])
    q = jnp.where(iota((half, half), 0) == map_ref[...], 1.0, 0.0).astype(F32)
    move_ref[0] = fdot(fdot(q, shared), q, NT)
    move_ref[1] = fdot(q, cross)
    mm_ref[...] = fdot(fdot(q, mass_shared), q, NT)


def faces(w, k, stiff, mass, bound, mapping):
    half = stiff.shape[0] // 2
    block = jax.ShapeDtypeStruct((half, half), F32)
    return pl.pallas_call(
        faces_kernel,
        out_shape=[block, jax.ShapeDtypeStruct((2, half, half), F32), block, block],
        compiler_params=pltpu.CompilerParams(vmem_limit_bytes=VMEM_LIMIT),
        name="faces",
    )(w, k, stiff, mass, bound, mapping)


def sweep(a, size):
    width = a.shape[1]
    lane = iota(a.shape, 1)
    row_at = iota(a.shape, 0)
    groups = width // size
    for k in range(size):
        col = a[:, k : k + 1]
        pivot = a[k : k + 1, k : k + 1]
        here = lane == k
        if groups == 1:
            col = jnp.broadcast_to(col, a.shape)
            pivot = jnp.broadcast_to(pivot, (1, width))
        else:
            col = jnp.where(lane < size, col, a[:, size + k : size + k + 1])
            pivot = jnp.where(lane[:1] < size, pivot, a[k : k + 1, size + k : size + k + 1])
            here = (lane == k) | (lane == size + k)
        scale = 1.0 / pivot
        row = jnp.where(here[:1], scale, a[k : k + 1, :] * scale)
        a = jnp.where(row_at == k, row, jnp.where(here, 0.0, a) - col * row)
    return a


def invert(ref, step):
    n = ref.shape[0]
    for p in range(n // step):
        at = slice(p * step, (p + 1) * step)
        pin = sweep(ref[at, at], step)
        panel = ref[at, :]
        col = ref[:, at]
        inside = (iota((step, n), 1) // step) == p
        row = jnp.where(inside, 0.0, fdot(pin, panel))
        left = (iota((n, step), 0) // step) == p
        colz = jnp.where(left, 0.0, col)
        ref[...] = ref[...] - fdot(colz, row)
        ref[:, at] = -fdot(colz, pin)
        ref[at, :] = row
        ref[at, at] = pin


STEP = 64


def begin_kernel(own_ref, move_ref, loads_ref, red_ref, inv_ref, z_ref, work):
    reduced = own_ref[...] + move_ref[0]
    red_ref[...] = reduced
    work[...] = reduced
    invert(work, STEP)
    inv_ref[...] = work[...]
    z_ref[...] = fdot(loads_ref[...], work[...])


def begin(own, moved, loads):
    half = own.shape[0]
    block = jax.ShapeDtypeStruct((half, half), F32)
    return pl.pallas_call(
        begin_kernel,
        out_shape=[block, block, jax.ShapeDtypeStruct(loads.shape, F32)],
        scratch_shapes=[pltpu.VMEM((half, half), F32)],
        compiler_params=pltpu.CompilerParams(vmem_limit_bytes=VMEM_LIMIT),
        name="begin",
    )(own, moved, loads)


def finish_kernel(g_ref, z_ref, sy_ref, out_ref):
    n = z_ref.shape[0]
    rho, gamma, kappa, delta = (g_ref[i] for i in range(4))
    both = sweep(jnp.concatenate([gamma, rho], axis=1), n)
    gamma_inv, rho_inv = both[:, :n], both[:, n:]
    c1 = fdot(gamma_inv, rho)
    cross = fdot(gamma, c1)
    rho_next = rho - cross - cross.T + fdot(c1, fdot(kappa, c1), TN)
    beta = fdot(rho_inv, rho_next)
    eye = jnp.where(iota((n, n), 0) == iota((n, n), 1), 1.0, 0.0)
    pb = eye + beta
    mixed = fdot(pb, fdot(kappa, c1), TN)
    gamma2 = fdot(pb, fdot(gamma, pb), TN) - mixed - mixed.T + fdot(c1, fdot(delta, c1), TN)
    c2 = fdot(sweep(gamma2, n), rho_next)
    out_ref[...] = fdot(c1 + fdot(pb, c2), z_ref[...], TN) - fdot(fdot(c1, c2), sy_ref[...], TN)


def finish(grams, z, sy):
    return pl.pallas_call(
        finish_kernel,
        out_shape=jax.ShapeDtypeStruct(z.shape, F32),
        compiler_params=pltpu.CompilerParams(vmem_limit_bytes=VMEM_LIMIT),
        name="finish",
    )(grams, z, sy)


def passed_along(array, axis, by):
    size = lax.axis_size(axis)
    return lax.ppermute(array, axis, [(i, (i + by) % size) for i in range(size)])


def summed(array, axis):
    size = lax.axis_size(axis)
    bit = 1
    while bit < size:
        array = array + lax.ppermute(array, axis, [(i, i ^ bit) for i in range(size)])
        bit *= 2
    return array


def shards(
    interior_factor, coupling, boundary_stiffness, interior_mass, boundary_mass, dof_map, load_cases
):
    w_own, k_own = modes(interior_factor[0], coupling[0])
    stiff = lax.all_gather(boundary_stiffness[0], "grp", axis=0, tiled=True)
    bound = lax.all_gather(boundary_mass[0], "grp", axis=0, tiled=True)
    w = lax.all_gather(w_own, "grp", axis=0, tiled=True)
    k = lax.all_gather(k_own, "grp", axis=0, tiled=True)
    own, move, own_mass, move_mass = faces(
        w, k, stiff, interior_mass, bound[None], dof_map
    )
    moved = passed_along(move, "sub", -1)
    moved_mass = passed_along(move_mass, "sub", -1)
    loads = load_cases[0]
    reduced, inverse, z = begin(own, moved, loads)

    def operate(v):
        return (
            fdot(v, reduced)
            + fdot(passed_along(v, "sub", 1), move[1])
            + fdot(passed_along(v, "sub", -1), moved[1], NT)
        )

    y = operate(z)
    sy = fdot(y, inverse)
    y2 = operate(sy)
    grams = summed(
        jnp.stack([fdot(loads, z, NT), fdot(z, y, NT), fdot(y, sy, NT), fdot(sy, y2, NT)]), "sub"
    )
    return (reduced[None], (own_mass + moved_mass)[None], finish(grams, z, sy)[None])


def solution(mesh):
    return jax.shard_map(
        shards,
        mesh=mesh,
        in_specs=(
            P("sub", None, None),
            P("sub", "grp", None),
            P("sub", "grp", None),
            P("sub", None),
            P("sub", "grp"),
            P("sub", None),
            P("sub", None, None),
        ),
        out_specs=(P("sub", None, None), P("sub", None, None), P("sub", None, None)),
        check_vma=False,
    )
```

time: 514 us -> 167 us (0.32); the launches traced: 505 us -> 167 us
  other arithmetic: 178 us -> 0.83 us
  blocking collectives: 83.8 us -> 1.92 us
  Pallas kernels: 0 us -> 57 us
  waiting for transfers between devices: 119 us -> 68.9 us
  matrix products: 48.4 us -> 3.74 us
  local copies, waits for them, and re-layouts: 42.1 us -> 6.32 us
    another operation x28 -> x1, other arithmetic: 173 us -> 0.01 us  [shards(): jnp.stack([fdot(loads, z, NT), fdot(z, y, NT), fdot(y, sy, NT), fdot(sy,...]
    psum x1 -> x0, waiting for transfers between devices: 96.9 us -> none  [shards(): rho_sum = lax.psum(inner_block(residual, smoothed), 'sub')]
    psum x1 -> x0, blocking collectives: 75.4 us -> none  [shards(): lax.psum((inner_block(direction, images), inner_block(residual, smoothed_...]
    pallas_call x0 -> x4, Pallas kernels: none -> 57 us  [the longest x1 25.7 us: begin(): pl.pallas_call(begin_kernel, out_shape=[block, block, jax.ShapeDtypeStruc...]
    another operation x50 -> x0, matrix products: 34.6 us -> none  [the longest x15 16.2 us: shards(): jax.scipy.linalg.solve_triangular(factor, coupling[0].astype(jnp.float32)...]
    another operation x38 -> x0, local copies, waits for them, and re-layouts: 27.6 us -> none
    ppermute x0 -> x4, waiting for transfers between devices: none -> 21.9 us  [summed(): lax.ppermute(array, axis, [(i, i ^ bit) for i in range(size)])]
    all_gather x2 -> x3, waiting for transfers between devices: 0.02 us -> 21 us  [the longest x1 11.8 us: shards(): k = lax.all_gather(k_own, 'grp', axis=0, tiled=True)]
  transfers between devices with their start and end apart: 9 -> 13, of which waited for: 6 -> 11; matrix products, arithmetic and copies ran while one was open for 12% -> 1% of each run, Pallas kernels for 0% -> 9%
where the time goes in v1:
time: 167 us
  waiting for transfers between devices  68.9 us (41%)
  Pallas kernels  57 us (34%)
  starting transfers between devices  14.5 us (9%)
  between operations  14 us (8%)
  local copies, waits for them, and re-layouts  6.32 us (4%)
  matrix products  3.74 us (2%)
  blocking collectives  1.92 us (1%)
    pallas_call x1, Pallas kernels, begin(): pl.pallas_call(begin_kernel, out_shape=[block, block, jax.ShapeDtypeStruc...  25.7 us
    ppermute x6, waiting for transfers between devices, passed_along(): lax.ppermute(array, axis, [(i, (i + by) % size) for i in range(size)])  24.7 us
    ppermute x4, waiting for transfers between devices, summed(): lax.ppermute(array, axis, [(i, i ^ bit) for i in range(size)])  21.9 us
    pallas_call x1, Pallas kernels, modes(): pl.pallas_call(modes_kernel, out_shape=[jax.ShapeDtypeStruct((width, ni),...  14.8 us
    ppermute x6, starting transfers between devices, passed_along(): lax.ppermute(array, axis, [(i, (i + by) % size) for i in range(size)])  14.1 us
    pallas_call x1, Pallas kernels, finish(): pl.pallas_call(finish_kernel, out_shape=jax.ShapeDtypeStruct(z.shape, F32...  13.6 us
    all_gather x1, waiting for transfers between devices, shards(): k = lax.all_gather(k_own, 'grp', axis=0, tiled=True)  11.8 us
    all_gather x1, waiting for transfers between devices, shards(): w = lax.all_gather(w_own, 'grp', axis=0, tiled=True)  9.22 us
  transfers between devices with their start and end apart: 13, of which 11 were waited for; matrix products, arithmetic and copies ran while one was open for 1% of the time, Pallas kernels for 9%

profile of v1, /device:TPU:0, one launch (start us, length us, event | category | flops | bytes accessed | tf_op | source)
XLA Modules:
  0.0 167.1 jit_solution(2272407130795900581)
XLA Ops:
  8.0 1.6 copy-done
  10.6 14.8 %modes.1 = (bf16[256,1024]{1,0:T(8,128)(2,1)}, bf16[256,1024]{1,0:T(8,128)(2,1)}) custom-call(bf16[1024,1024]{1,0:T(8,128)(2,1)S(1)} %bitcast.46, bf16[256,1024]{1,0:T(8,128)(2,1)S(1)} %bitcast.48), custom_call_target="tpu_custom_call" | custom-call | tf_op jit(solution)/shard_map/modes/pallas_call | solution.py:106
  26.2 1.9 %all-gather.1.bound_ref = f32[1,512]{1,0:T(1,128)S(1)} all-gather(f32[1,256]{1,0:T(1,128)S(1)} %copy-done.9), channel_id=3, replica_groups=mesh['sub'=16,'grp'=2] {'grp'}, dimensions={1}, use_global_device_ids=true | all-gather | bytes 3072 | tf_op jit(solution)/shard_map/all_gather | solution.py:259
  28.1 9.2 %all-gather.6.cloned.1.call-done.w_ref = bf16[512,1024]{1,0:T(8,128)(2,1)} async-done(((bf16[256,1024]{1,0:T(8,128)(2,1)}), bf16[512,1024]{1,0:T(8,128)(2,1)}) %all-gather.6.cloned.1.call-update) | async-done | bytes 1048592 | tf_op jit(solution)/shard_map/all_gather | solution.py:260
  37.3 11.8 %all-gather.8.cloned.1.call-done.k_ref = bf16[512,1024]{1,0:T(8,128)(2,1)} async-done(((bf16[256,1024]{1,0:T(8,128)(2,1)}), bf16[512,1024]{1,0:T(8,128)(2,1)}) %all-gather.8.cloned.1.call-update) | async-done | bytes 1048592 | tf_op jit(solution)/shard_map/all_gather | solution.py:261
  49.1 1.2 copy-done.1
  50.4 1.2 copy-done.2
  51.6 1.2 copy-done.3
  52.8 2.8 %faces.1 = (f32[256,256]{1,0:T(8,128)S(1)}, f32[2,256,256]{2,1,0:T(8,128)S(1)}, f32[256,256]{1,0:T(8,128)S(1)}, f32[256,256]{1,0:T(8,128)S(1)}) custom-call(bf16[512,1024]{1,0:T(8,128)(2,1)S(1)} %copy-done.2, bf16[512,1024]{1,0:T(8,128)(2,1)S(1)} %copy-done.3, f32[512,512]{1,0:T(8,128)S(1)} %bitcast.47, f32[1,1024]{1,0:T(1,128)S(1)} %copy-done.6, ...), custom_call_target="tpu_custom_call" | custom-call | tf_op jit(solution)/shard_map/faces/pallas_call | solution.py:143
  55.6 5.6 %collective-permute-start = (f32[2,256,256]{2,1,0:T(8,128)S(1)}, f32[2,256,256]{2,1,0:T(8,128)S(1)}, u32[]{:S(2)}, u32[]{:S(2)}) collective-permute-start(f32[2,256,256]{2,1,0:T(8,128)S(1)} %get-tuple-element.15), channel_id=1, source_target_pairs={{0,30},{2,0},{4,2},{6,4},{8,6},{10,8},{12,10},{14,12},{16,14},{18,... | collective-permute-start | bytes 1572872 | tf_op jit(solution)/shard_map/ppermute | solution.py:242
  61.2 11.7 %collective-permute-done.move_ref = f32[2,256,256]{2,1,0:T(8,128)S(1)} collective-permute-done((f32[2,256,256]{2,1,0:T(8,128)S(1)}, f32[2,256,256]{2,1,0:T(8,128)S(1)}, u32[]{:S(2)}, u32[]{:S(2)}) %collective-permute-start) | collective-permute-done | bytes 524320 | tf_op jit(solution)/shard_map/ppermute | solution.py:242
  72.9 25.7 %begin.1 = (f32[256,256]{1,0:T(8,128)}, f32[256,256]{1,0:T(8,128)S(1)}, f32[64,256]{1,0:T(8,128)S(1)}) custom-call(f32[256,256]{1,0:T(8,128)S(1)} %get-tuple-element.14.own_ref, f32[2,256,256]{2,1,0:T(8,128)S(1)} %collective-permute-done.move_ref, f32[64,256]{1,0:T(8,128)S(1)} %bitcast.49), custom_call_target="tpu_custom_call" | custom-call | tf_op jit(solution)/shard_map/begin/pallas_call | solution.py:205
  98.6 6.1 %collective-permute-start.3 = (f32[64,256]{1,0:T(8,128)S(1)}, f32[64,256]{1,0:T(8,128)S(1)}, u32[]{:S(2)}, u32[]{:S(2)}) collective-permute-start(f32[64,256]{1,0:T(8,128)S(1)} %get-tuple-element.19.z_ref), channel_id=1, source_target_pairs={{0,30},{2,0},{4,2},{6,4},{8,6},{10,8},{12,10},{14,12},{16,14},{18,... | collective-permute-start | bytes 196616 | tf_op jit(solution)/shard_map/ppermute | solution.py:242
  104.9 1.7 %collective-permute-done.3 = f32[64,256]{1,0:T(8,128)S(1)} collective-permute-done((f32[64,256]{1,0:T(8,128)S(1)}, f32[64,256]{1,0:T(8,128)S(1)}, u32[]{:S(2)}, u32[]{:S(2)}) %collective-permute-start.3) | collective-permute-done | bytes 65568 | tf_op jit(solution)/shard_map/ppermute | solution.py:242
  107.0 5.6 %collective-permute-done.2 = f32[64,256]{1,0:T(8,128)S(1)} collective-permute-done((f32[64,256]{1,0:T(8,128)S(1)}, f32[64,256]{1,0:T(8,128)S(1)}, u32[]{:S(2)}, u32[]{:S(2)}) %collective-permute-start.2) | collective-permute-done | bytes 65568 | tf_op jit(solution)/shard_map/ppermute | solution.py:242
  112.8 1.2 fusion.1
  114.9 1.6 collective-permute-start.4
  116.8 2.0 %collective-permute-done.5 = f32[64,256]{1,0:T(8,128)S(1)} collective-permute-done((f32[64,256]{1,0:T(8,128)S(1)}, f32[64,256]{1,0:T(8,128)S(1)}, u32[]{:S(2)}, u32[]{:S(2)}) %collective-permute-start.5) | collective-permute-done | bytes 65568 | tf_op jit(solution)/shard_map/ppermute | solution.py:242
  119.2 3.7 %collective-permute-done.4 = f32[64,256]{1,0:T(8,128)S(1)} collective-permute-done((f32[64,256]{1,0:T(8,128)S(1)}, f32[64,256]{1,0:T(8,128)S(1)}, u32[]{:S(2)}, u32[]{:S(2)}) %collective-permute-start.4) | collective-permute-done | bytes 65568 | tf_op jit(solution)/shard_map/ppermute | solution.py:242
  123.7 6.3 %collective-permute-done.6 = f32[4,64,64]{2,1,0:T(8,128)S(1)} collective-permute-done((f32[4,64,64]{2,1,0:T(8,128)S(1)}, f32[4,64,64]{2,1,0:T(8,128)S(1)}, u32[]{:S(2)}, u32[]{:S(2)}) %collective-permute-start.6) | collective-permute-done | bytes 65568 | tf_op jit(solution)/shard_map/ppermute | solution.py:249
  130.4 4.7 %collective-permute-done.7 = f32[4,64,64]{2,1,0:T(8,128)S(1)} collective-permute-done((f32[4,64,64]{2,1,0:T(8,128)S(1)}, f32[4,64,64]{2,1,0:T(8,128)S(1)}, u32[]{:S(2)}, u32[]{:S(2)}) %collective-permute-start.7) | collective-permute-done | bytes 65568 | tf_op jit(solution)/shard_map/ppermute | solution.py:249
  135.2 5.0 %collective-permute-done.8 = f32[4,64,64]{2,1,0:T(8,128)S(1)} collective-permute-done((f32[4,64,64]{2,1,0:T(8,128)S(1)}, f32[4,64,64]{2,1,0:T(8,128)S(1)}, u32[]{:S(2)}, u32[]{:S(2)}) %collective-permute-start.8) | collective-permute-done | bytes 65568 | tf_op jit(solution)/shard_map/ppermute | solution.py:249
  141.0 5.9 %collective-permute-done.9 = f32[4,64,64]{2,1,0:T(8,128)S(1)} collective-permute-done((f32[4,64,64]{2,1,0:T(8,128)S(1)}, f32[4,64,64]{2,1,0:T(8,128)S(1)}, u32[]{:S(2)}, u32[]{:S(2)}) %collective-permute-start.9) | collective-permute-done | bytes 65568 | tf_op jit(solution)/shard_map/ppermute | solution.py:249
  147.0 13.6 %finish.1 = f32[64,256]{1,0:T(8,128)} custom-call(f32[4,64,64]{2,1,0:T(8,128)S(1)} %add.35.g_ref, f32[64,256]{1,0:T(8,128)S(1)} %get-tuple-element.19.z_ref, f32[64,256]{1,0:T(8,128)S(1)} %fusion.12.sy_ref), custom_call_target="tpu_custom_call" | custom-call | tf_op jit(solution)/shard_map/finish/pallas_call | solution.py:232
  (47 shorter events, 6.9 us)
Async XLA Ops:
  7.2 19.0 %copy-start.9 = (f32[1,256]{1,0:T(1,128)S(1)}, f32[1,256]{1,0:T(1,128)}, u32[]{:S(2)}) copy-start(f32[1,256]{1,0:T(1,128)} %param.11) | copy-start | bytes 3076
  7.2 42.0 %copy-start.7 = (s32[1,256]{1,0:T(1,128)S(1)}, s32[1,256]{1,0:T(1,128)}, u32[]{:S(2)}) copy-start(s32[1,256]{1,0:T(1,128)} %map_ref.1) | copy-start | bytes 3076
  7.2 41.9 %copy-start.6 = (f32[1,1024]{1,0:T(1,128)S(1)}, f32[1,1024]{1,0:T(1,128)}, u32[]{:S(2)}) copy-start(f32[1,1024]{1,0:T(1,128)} %mass_ref.1) | copy-start | bytes 12292
  7.2 20.9 %all-gather.10.cloned.1.call-start = ((), (), s32[]{:S(2)}) async-start(), calls=%async_computation.2 | async-start | bytes 1572864 | tf_op jit(solution)/shard_map/all_gather | solution.py:258
  7.9 29.4 %all-gather.6.cloned.1.call-start = ((), (), s32[]{:S(2)}) async-start(), calls=%async_computation | async-start | bytes 1572864 | tf_op jit(solution)/shard_map/all_gather | solution.py:260
  8.0 1.6 copy-start
  9.6 1.0 copy-start.4
  25.4 47.5 %copy-start.5 = (f32[1,64,256]{2,1,0:T(8,128)S(1)}, f32[1,64,256]{2,1,0:T(8,128)}, u32[]{:S(2)}) copy-start(f32[1,64,256]{2,1,0:T(8,128)} %param.13) | copy-start | bytes 196612
  25.5 23.7 %all-gather.8.cloned.1.call-start = ((), (), s32[]{:S(2)}) async-start(), calls=%async_computation.1 | async-start | bytes 1572864 | tf_op jit(solution)/shard_map/all_gather | solution.py:261
  49.1 1.2 copy-start.1
  50.4 1.2 copy-start.2
  51.6 1.2 copy-start.3
  55.6 17.3 %collective-permute-start = (f32[2,256,256]{2,1,0:T(8,128)S(1)}, f32[2,256,256]{2,1,0:T(8,128)S(1)}, u32[]{:S(2)}, u32[]{:S(2)}) collective-permute-start(f32[2,256,256]{2,1,0:T(8,128)S(1)} %get-tuple-element.15), channel_id=1, source_target_pairs={{0,30},{2,0},{4,2},{6,4},{8,6},{10,8},{12,10},{14,12},{16,14},{18,... | collective-permute-start | bytes 1572872 | tf_op jit(solution)/shard_map/ppermute | solution.py:242
  98.6 24.5 %copy-start.8 = (f32[256,256]{1,0:T(8,128)S(1)}, f32[256,256]{1,0:T(8,128)}, u32[]{:S(2)}) copy-start(f32[256,256]{1,0:T(8,128)} %get-tuple-element.16) | copy-start | bytes 786436
  98.6 8.0 %collective-permute-start.3 = (f32[64,256]{1,0:T(8,128)S(1)}, f32[64,256]{1,0:T(8,128)S(1)}, u32[]{:S(2)}, u32[]{:S(2)}) collective-permute-start(f32[64,256]{1,0:T(8,128)S(1)} %get-tuple-element.19.z_ref), channel_id=1, source_target_pairs={{0,30},{2,0},{4,2},{6,4},{8,6},{10,8},{12,10},{14,12},{16,14},{18,... | collective-permute-start | bytes 196616 | tf_op jit(solution)/shard_map/ppermute | solution.py:242
  104.7 7.9 %collective-permute-start.2 = (f32[64,256]{1,0:T(8,128)S(1)}, f32[64,256]{1,0:T(8,128)S(1)}, u32[]{:S(2)}, u32[]{:S(2)}) collective-permute-start(f32[64,256]{1,0:T(8,128)S(1)} %get-tuple-element.19.z_ref), channel_id=1, source_target_pairs={{0,2},{2,4},{4,6},{6,8},{8,10},{10,12},{12,14},{14,16},{16,18},{18... | collective-permute-start | bytes 196616 | tf_op jit(solution)/shard_map/ppermute | solution.py:242
  114.5 4.3 %collective-permute-start.5 = (f32[64,256]{1,0:T(8,128)S(1)}, f32[64,256]{1,0:T(8,128)S(1)}, u32[]{:S(2)}, u32[]{:S(2)}) collective-permute-start(f32[64,256]{1,0:T(8,128)S(1)} %fusion.12.sy_ref), channel_id=1, source_target_pairs={{0,30},{2,0},{4,2},{6,4},{8,6},{10,8},{12,10},{14,12},{16,14},{18,... | collective-permute-start | bytes 196616 | tf_op jit(solution)/shard_map/ppermute | solution.py:242
  114.9 8.0 %collective-permute-start.4 = (f32[64,256]{1,0:T(8,128)S(1)}, f32[64,256]{1,0:T(8,128)S(1)}, u32[]{:S(2)}, u32[]{:S(2)}) collective-permute-start(f32[64,256]{1,0:T(8,128)S(1)} %fusion.12.sy_ref), channel_id=1, source_target_pairs={{0,2},{2,4},{4,6},{6,8},{8,10},{10,12},{12,14},{14,16},{16,18},{18... | collective-permute-start | bytes 196616 | tf_op jit(solution)/shard_map/ppermute | solution.py:242
  123.7 6.4 %collective-permute-start.6 = (f32[4,64,64]{2,1,0:T(8,128)S(1)}, f32[4,64,64]{2,1,0:T(8,128)S(1)}, u32[]{:S(2)}, u32[]{:S(2)}) collective-permute-start(f32[4,64,64]{2,1,0:T(8,128)S(1)} %pad_maximum_fusion), channel_id=1, source_target_pairs={{0,2},{2,0},{4,6},{6,4},{8,10},{10,8},{12,14},{14,12},{16,18},{18,... | collective-permute-start | bytes 196616 | tf_op jit(solution)/shard_map/ppermute | solution.py:249
  130.1 5.0 %collective-permute-start.7 = (f32[4,64,64]{2,1,0:T(8,128)S(1)}, f32[4,64,64]{2,1,0:T(8,128)S(1)}, u32[]{:S(2)}, u32[]{:S(2)}) collective-permute-start(f32[4,64,64]{2,1,0:T(8,128)S(1)} %fusion.11), channel_id=1, source_target_pairs={{0,4},{2,6},{4,0},{6,2},{8,12},{10,14},{12,8},{14,10},{16,20},{18,... | collective-permute-start | bytes 196616 | tf_op jit(solution)/shard_map/ppermute | solution.py:249
  130.2 10.1 %collective-permute-start.1 = (f32[256,256]{1,0:T(8,128)S(1)}, f32[256,256]{1,0:T(8,128)S(1)}, u32[]{:S(2)}, u32[]{:S(2)}) collective-permute-start(f32[256,256]{1,0:T(8,128)S(1)} %get-tuple-element.18), channel_id=1, source_target_pairs={{0,30},{2,0},{4,2},{6,4},{8,6},{10,8},{12,10},{14,12},{16,14},{18,... | collective-permute-start | bytes 786440 | tf_op jit(solution)/shard_map/ppermute | solution.py:242
  135.1 5.0 %collective-permute-start.8 = (f32[4,64,64]{2,1,0:T(8,128)S(1)}, f32[4,64,64]{2,1,0:T(8,128)S(1)}, u32[]{:S(2)}, u32[]{:S(2)}) collective-permute-start(f32[4,64,64]{2,1,0:T(8,128)S(1)} %fusion.30), channel_id=1, source_target_pairs={{0,8},{2,10},{4,12},{6,14},{8,0},{10,2},{12,4},{14,6},{16,24},{18,... | collective-permute-start | bytes 196616 | tf_op jit(solution)/shard_map/ppermute | solution.py:249
  140.2 6.8 %collective-permute-start.9 = (f32[4,64,64]{2,1,0:T(8,128)S(1)}, f32[4,64,64]{2,1,0:T(8,128)S(1)}, u32[]{:S(2)}, u32[]{:S(2)}) collective-permute-start(f32[4,64,64]{2,1,0:T(8,128)S(1)} %add.34), channel_id=1, source_target_pairs={{0,16},{2,18},{4,20},{6,22},{8,24},{10,26},{12,28},{14,30},{16,0},... | collective-permute-start | bytes 196616 | tf_op jit(solution)/shard_map/ppermute | solution.py:249
Sparse Core Ops, SparseCore 0:
  9.6 11.7 all-gather.9
  25.6 11.7 all-gather.5
  38.9 10.1 all-gather.7

commit v2 on v1

v2 whole, which is shorter than its diff:
```python
import functools
import jax
import jax.numpy as jnp
from jax import lax
from jax.experimental import pallas as pl
from jax.experimental.pallas import tpu as pltpu
from jax.sharding import PartitionSpec as P

F32 = jnp.float32
BF16 = jnp.bfloat16
HIGH = lax.Precision.HIGHEST
TILE = 128
VMEM_LIMIT = 48 * 2**20
NT = (((1,), (1,)), ((), ()))
NN = (((1,), (0,)), ((), ()))
TN = (((0,), (0,)), ((), ()))


def dot(a, b, dims=NN):
    return lax.dot_general(a, b, dims, preferred_element_type=F32)


def fdot(a, b, dims=NN):
    return lax.dot_general(a, b, dims, precision=HIGH, preferred_element_type=F32)


def split(x):
    hi = x.astype(BF16)
    return hi, (x - hi.astype(F32)).astype(BF16)


def dot3(a, b, dims=NN):
    ah, al = split(a)
    bh, bl = split(b)
    return dot(ah, bh, dims) + (dot(ah, bl, dims) + dot(al, bh, dims))


def iota(shape, dim):
    return lax.broadcasted_iota(jnp.int32, shape, dim)


def solve_modes(l_ref, c_ref, put, inv, wh, wl):
    ni = l_ref.shape[0]
    count = ni // TILE
    rows = iota((TILE, TILE), 0)
    cols = iota((TILE, TILE), 1)

    def block(j):
        return l_ref[j * TILE : (j + 1) * TILE, j * TILE : (j + 1) * TILE]

    pair = ((rows >> 1) == (cols >> 1)) & (rows > cols)
    for j in range(count):
        full = block(j).astype(F32)
        diag = jnp.where(rows == cols, full, 0.0)
        down = 1.0 / jnp.sum(diag, axis=1, keepdims=True)
        across = 1.0 / jnp.sum(diag, axis=0, keepdims=True)
        first = jnp.where(rows == cols, down, 0.0)
        inv[j] = first - jnp.where(pair, down * full * across, 0.0)

    levels = TILE.bit_length() - 1

    def level(lev, carry):
        same = (rows >> (lev + 1)) == (cols >> (lev + 1))
        low = ((rows >> lev) & 1) > ((cols >> lev) & 1)
        mask = same & low
        for j in range(count):
            x = inv[j]
            off = jnp.where(mask, block(j).astype(F32), 0.0).astype(BF16)
            xh, xl = split(x)
            mid = dot(xh, off) + dot(xl, off)
            mh, ml = split(mid)
            inv[j] = x - (dot(mh, xh) + (dot(mh, xl) + dot(ml, xh)))
        return carry

    lax.fori_loop(1, levels, level, 0)

    for j in range(count):
        at = slice(j * TILE, (j + 1) * TILE)
        acc = c_ref[:, at].astype(F32)
        if j:
            before = slice(0, j * TILE)
            acc = acc - (
                dot(wh[:, before], l_ref[at, before], NT)
                + dot(wl[:, before], l_ref[at, before], NT)
            )
        piece = dot3(acc, inv[j], NT)
        hi, lo = split(piece)
        wh[:, at] = hi
        wl[:, at] = lo
    put(0)
    for j in reversed(range(count)):
        at = slice(j * TILE, (j + 1) * TILE)
        acc = wh[:, at].astype(F32) + wl[:, at].astype(F32)
        if j + 1 < count:
            after = slice((j + 1) * TILE, ni)
            acc = acc + (dot(wh[:, after], l_ref[after, at]) + dot(wl[:, after], l_ref[after, at]))
        piece = -dot3(acc, inv[j])
        hi, lo = split(piece)
        wh[:, at] = hi
        wl[:, at] = lo
    put(1)


def at_device(sub, grp):
    return dict(device_id=(sub, grp), device_id_type=pl.DeviceIdType.MESH)


def substructure_kernel(
    l_ref, c_ref, rows_ref, mass_ref, bound_ref, map_ref,
    own_ref, move_ref, om_ref, mm_ref,
    inv, wh, wl, both, stiff, bound, send, recv,
):
    grp = lax.axis_index("grp")
    sub = lax.axis_index("sub")
    members = lax.axis_size("grp")
    width = c_ref.shape[0]
    mine = pl.ds(pl.multiple_of(grp * width, width), width)
    others = [lax.rem(grp + d, members) for d in range(1, members)]

    barrier = pltpu.get_barrier_semaphore()
    for other in others:
        pl.semaphore_signal(barrier, inc=1, **at_device(sub, other))
    pl.semaphore_wait(barrier, members - 1)

    copies = []

    def spread(item, src, dst):
        for d, other in enumerate(others):
            copy = pltpu.make_async_remote_copy(
                src_ref=src, dst_ref=dst,
                send_sem=send.at[item, d], recv_sem=recv.at[item, d],
                **at_device(sub, other),
            )
            copy.start()
            copies.append(copy)

    spread(2, rows_ref, stiff.at[mine])
    spread(3, bound_ref, bound.at[grp])
    stiff[mine, :] = rows_ref[...]
    bound[grp] = bound_ref[...]

    def put(item):
        both[item, mine, :] = wh[...]
        spread(item, both.at[item, mine], both.at[item, mine])

    solve_modes(l_ref, c_ref, put, inv, wh, wl)
    for copy in copies:
        copy.wait()

    half = rows_ref.shape[1] // 2
    wo, ws = both[0, :half], both[0, half:]
    own_ref[...] = stiff[:half, :half] - dot(wo, wo, NT)
    shared = stiff[half:, half:] - dot(ws, ws, NT)
    cross = stiff[half:, :half] - dot(ws, wo, NT)
    weights = mass_ref[...]
    eye = iota((half, half), 0) == iota((half, half), 1)
    pieces = jnp.concatenate([bound[i] for i in range(members)], axis=1)

    def mass_of(c, b):
        ch, cl = split(c.astype(F32) * weights)
        return dot(ch, c, NT) + dot(cl, c, NT) + jnp.where(eye, b, 0.0)

    om_ref[...] = mass_of(both[1, :half], pieces[:, :half])
    mass_shared = mass_of(both[1, half:], pieces[:, half:])
    q = jnp.where(iota((half, half), 0) == map_ref[...], 1.0, 0.0).astype(F32)
    move_ref[0] = fdot(fdot(q, shared), q, NT)
    move_ref[1] = fdot(q, cross)
    mm_ref[...] = fdot(fdot(q, mass_shared), q, NT)


def substructure(factor, coupling, rows, mass, bound, mapping):
    width, ni = coupling.shape
    nbound = rows.shape[1]
    half = nbound // 2
    members = nbound // width
    block = jax.ShapeDtypeStruct((half, half), F32)
    peers = max(members - 1, 1)
    return pl.pallas_call(
        substructure_kernel,
        out_shape=[block, jax.ShapeDtypeStruct((2, half, half), F32), block, block],
        in_specs=[pl.BlockSpec(memory_space=pltpu.VMEM)] * 6,
        out_specs=[pl.BlockSpec(memory_space=pltpu.VMEM)] * 4,
        scratch_shapes=[
            pltpu.VMEM((ni // TILE, TILE, TILE), F32),
            pltpu.VMEM((width, ni), BF16),
            pltpu.VMEM((width, ni), BF16),
            pltpu.VMEM((2, nbound, ni), BF16),
            pltpu.VMEM((nbound, nbound), F32),
            pltpu.VMEM((members, 1, width), F32),
            pltpu.SemaphoreType.DMA((4, peers)),
            pltpu.SemaphoreType.DMA((4, peers)),
        ],
        compiler_params=pltpu.CompilerParams(
            vmem_limit_bytes=VMEM_LIMIT, collective_id=0, has_side_effects=True
        ),
        name="substructure",
    )(factor, coupling, rows, mass, bound, mapping)


def sweep(a, size):
    width = a.shape[1]
    lane = iota(a.shape, 1)
    lane_row = lane[:1]
    row_at = iota(a.shape, 0)
    first = lane < size

    def lanes(rows, k):
        if width == size:
            return jnp.broadcast_to(rows[:, k : k + 1], rows.shape)
        left = rows[:, k : k + 1]
        right = rows[:, size + k : size + k + 1]
        return jnp.where(first[: rows.shape[0]], left, right)

    local = jnp.where(first, lane, lane - size)
    local_row = local[:1]
    for k in range(0, size, 2):
        c0, c1 = lanes(a, k), lanes(a, k + 1)
        r0, r1 = a[k : k + 1, :], a[k + 1 : k + 2, :]
        p, q, s = c0[k : k + 1], c1[k : k + 1], c1[k + 1 : k + 2]
        scale = 1.0 / (p * s - q * q)
        ip, iq, ir = s * scale, -q * scale, p * scale
        at0, at1 = local_row == k, local_row == k + 1
        n0 = jnp.where(at0, ip, jnp.where(at1, iq, ip * r0 + iq * r1))
        n1 = jnp.where(at0, iq, jnp.where(at1, ir, iq * r0 + ir * r1))
        inside = (local >> 1) == (k >> 1)
        a = jnp.where(inside, 0.0, a) - c0 * n0 - c1 * n1
        a = jnp.where(row_at == k, n0, jnp.where(row_at == k + 1, n1, a))
    return a


def invert(ref, step):
    n = ref.shape[0]
    for p in range(n // step):
        at = slice(p * step, (p + 1) * step)
        pin = sweep(ref[at, at], step)
        panel = ref[at, :]
        col = ref[:, at]
        inside = (iota((step, n), 1) // step) == p
        row = jnp.where(inside, 0.0, fdot(pin, panel))
        left = (iota((n, step), 0) // step) == p
        colz = jnp.where(left, 0.0, col)
        ref[...] = ref[...] - fdot(colz, row)
        ref[:, at] = -fdot(colz, pin)
        ref[at, :] = row
        ref[at, at] = pin


STEP = 64


def stages_of(size):
    stages, stride = [], 1
    while stride < size:
        radix = 4 if stride * 4 <= size else 2
        stages.append((stride, radix))
        stride *= radix
    return stages


def interface_kernel(
    own_ref, move_ref, om_ref, mm_ref, loads_ref,
    red_ref, mass_ref, out_ref,
    came, came_cross, came_mass, work, z, sy, near, acc, got, total,
    part_send, part_recv, fwd_send, fwd_recv, big_send, big_recv,
    dir_send, dir_recv, sum_send, sum_recv, all_send, all_recv,
):
    grp, sub = lax.axis_index("grp"), lax.axis_index("sub")
    members, size = lax.axis_size("grp"), lax.axis_size("sub")
    ahead, back = lax.rem(sub + 1, size), lax.rem(sub + size - 1, size)
    others = [lax.rem(grp + d, members) for d in range(1, members)]
    half = own_ref.shape[0]
    n = loads_ref.shape[0]
    stages = stages_of(size)

    def partner(stride, radix, d):
        digit = lax.rem(lax.div(sub, stride), radix)
        return sub + (lax.rem(digit + d, radix) - digit) * stride

    barrier = pltpu.get_barrier_semaphore()
    greeted = 0
    for other in others:
        pl.semaphore_signal(barrier, inc=1, **at_device(sub, other))
        greeted += 1
    for to in [ahead, back] + [partner(t, r, d) for t, r in stages for d in range(1, r)]:
        pl.semaphore_signal(barrier, inc=1, **at_device(to, grp))
        greeted += 1
    pl.semaphore_wait(barrier, greeted)

    def remote(src, dst, send, recv, to_sub, to_grp):
        copy = pltpu.make_async_remote_copy(
            src_ref=src, dst_ref=dst, send_sem=send, recv_sem=recv, **at_device(to_sub, to_grp)
        )
        copy.start()
        return copy

    share = half // members
    part = pl.ds(pl.multiple_of(grp * share, share), share)
    first = remote(move_ref.at[0, part], came.at[part], part_send.at[0], part_recv.at[0], back, grp)
    first.wait()
    forwards = [
        remote(came.at[part], came.at[part], fwd_send.at[d], fwd_recv.at[d], sub, other)
        for d, other in enumerate(others)
    ]
    cross_copy = remote(move_ref.at[1], came_cross, big_send.at[0], big_recv.at[0], back, grp)
    for copy in forwards:
        copy.wait()
    mass_copy = remote(mm_ref, came_mass, big_send.at[1], big_recv.at[1], back, grp)

    red_ref[...] = own_ref[...] + came[...]
    work[...] = red_ref[...]
    invert(work, STEP)
    z[...] = fdot(loads_ref[...], work[...])

    def neighbours(v, use):
        return [
            remote(v, near.at[use, 0], dir_send.at[use, 0], dir_recv.at[use, 0], ahead, grp),
            remote(v, near.at[use, 1], dir_send.at[use, 1], dir_recv.at[use, 1], back, grp),
        ]

    def from_neighbours(use):
        return fdot(near[use, 0], move_ref[1]) + fdot(near[use, 1], came_cross[...], NT)

    copies = neighbours(z, 0)
    y = fdot(z[...], red_ref[...])
    rho = fdot(loads_ref[...], z[...], NT)
    cross_copy.wait()
    for copy in copies:
        copy.wait()
    y = y + from_neighbours(0)
    sy[...] = fdot(y, work[...])
    copies = neighbours(sy, 1)
    y2 = fdot(sy[...], red_ref[...])
    gamma = fdot(z[...], y, NT)
    kappa = fdot(y, sy[...], NT)
    acc[0, :n, :n] = rho
    acc[0, :n, n:] = gamma
    acc[0, n:, :n] = kappa
    mass_copy.wait()
    mass_ref[...] = om_ref[...] + came_mass[...]
    for copy in copies:
        copy.wait()
    y2 = y2 + from_neighbours(1)
    acc[0, n:, n:] = fdot(sy[...], y2, NT)

    rows = 2 * n // members
    chunk = pl.ds(pl.multiple_of(grp * rows, rows), rows)
    slot = 0
    for i, (stride, radix) in enumerate(stages):
        copies = [
            remote(
                acc.at[i, chunk], got.at[slot + d - 1],
                sum_send.at[slot + d - 1], sum_recv.at[slot + d - 1],
                partner(stride, radix, d), grp,
            )
            for d in range(1, radix)
        ]
        value = acc[i, chunk, :]
        for d, copy in enumerate(copies):
            copy.wait()
            value = value + got[slot + d]
        acc[i + 1, chunk, :] = value
        slot += radix - 1
    last = len(stages)
    total[chunk, :] = acc[last, chunk, :]
    copies = [
        remote(acc.at[last, chunk], total.at[chunk], all_send.at[d], all_recv.at[d], sub, other)
        for d, other in enumerate(others)
    ]
    for copy in copies:
        copy.wait()

    rho, gamma = total[:n, :n], total[:n, n:]
    kappa, delta = total[n:, :n], total[n:, n:]
    both = sweep(jnp.concatenate([gamma, rho], axis=1), n)
    gamma_inv, rho_inv = both[:, :n], both[:, n:]
    c1 = fdot(gamma_inv, rho)
    cross = fdot(gamma, c1)
    rho_next = rho - cross - cross.T + fdot(c1, fdot(kappa, c1), TN)
    beta = fdot(rho_inv, rho_next)
    eye = jnp.where(iota((n, n), 0) == iota((n, n), 1), 1.0, 0.0)
    pb = eye + beta
    mixed = fdot(pb, fdot(kappa, c1), TN)
    gamma2 = fdot(pb, fdot(gamma, pb), TN) - mixed - mixed.T + fdot(c1, fdot(delta, c1), TN)
    c2 = fdot(sweep(gamma2, n), rho_next)
    out_ref[...] = fdot(c1 + fdot(pb, c2), z[...], TN) - fdot(fdot(c1, c2), sy[...], TN)


def interface(own, move, own_mass, move_mass, loads, size, members):
    half = own.shape[0]
    n = loads.shape[0]
    block = jax.ShapeDtypeStruct((half, half), F32)
    stages = stages_of(size)
    slots = sum(r - 1 for _, r in stages)
    peers = max(members - 1, 1)
    dma = pltpu.SemaphoreType.DMA
    return pl.pallas_call(
        interface_kernel,
        out_shape=[block, block, jax.ShapeDtypeStruct(loads.shape, F32)],
        in_specs=[pl.BlockSpec(memory_space=pltpu.VMEM)] * 5,
        out_specs=[pl.BlockSpec(memory_space=pltpu.VMEM)] * 3,
        scratch_shapes=[
            pltpu.VMEM((half, half), F32),
            pltpu.VMEM((half, half), F32),
            pltpu.VMEM((half, half), F32),
            pltpu.VMEM((half, half), F32),
            pltpu.VMEM((n, half), F32),
            pltpu.VMEM((n, half), F32),
            pltpu.VMEM((2, 2, n, half), F32),
            pltpu.VMEM((len(stages) + 1, 2 * n, 2 * n), F32),
            pltpu.VMEM((slots, 2 * n // members, 2 * n), F32),
            pltpu.VMEM((2 * n, 2 * n), F32),
            dma((1,)), dma((1,)), dma((peers,)), dma((peers,)), dma((2,)), dma((2,)),
            dma((2, 2)), dma((2, 2)), dma((slots,)), dma((slots,)), dma((peers,)), dma((peers,)),
        ],
        compiler_params=pltpu.CompilerParams(
            vmem_limit_bytes=VMEM_LIMIT, collective_id=1, has_side_effects=True
        ),
        name="interface",
    )(own, move, own_mass, move_mass, loads)


def shards(
    interior_factor, coupling, boundary_stiffness, interior_mass, boundary_mass, dof_map, load_cases
):
    own, move, own_mass, move_mass = substructure(
        interior_factor[0], coupling[0], boundary_stiffness[0], interior_mass, boundary_mass, dof_map
    )
    reduced, reduced_mass, found = interface(
        own, move, own_mass, move_mass, load_cases[0], lax.axis_size("sub"), lax.axis_size("grp")
    )
    return (reduced[None], reduced_mass[None], found[None])


def solution(mesh):
    return jax.shard_map(
        shards,
        mesh=mesh,
        in_specs=(
            P("sub", None, None),
            P("sub", "grp", None),
            P("sub", "grp", None),
            P("sub", None),
            P("sub", "grp"),
            P("sub", None),
            P("sub", None, None),
        ),
        out_specs=(P("sub", None, None), P("sub", None, None), P("sub", None, None)),
        check_vma=False,
    )
```

time: 167 us -> 89.5 us (0.54)
  waiting for transfers between devices: 68.9 us -> 0 us
  Pallas kernels: 57 us -> 80.7 us
  starting transfers between devices: 14.5 us -> 0 us
  between operations: 14 us -> 0.67 us
  matrix products: 3.74 us -> 0 us
  blocking collectives: 1.92 us -> 0 us
    ppermute x10 -> x0, waiting for transfers between devices: 46.6 us -> none  [the longest x6 24.7 us: passed_along(): lax.ppermute(array, axis, [(i, (i + by) % size) for i in range(size)])]
    pallas_call x4 -> x2, Pallas kernels: 57 us -> 80.7 us  [the longest x1 61.8 us: interface(): pl.pallas_call(interface_kernel, out_shape=[block, block, jax.ShapeDtypeS...]
    all_gather x3 -> x0, waiting for transfers between devices: 21 us -> none  [the longest x1 11.8 us: shards(): k = lax.all_gather(k_own, 'grp', axis=0, tiled=True)]
    ppermute x10 -> x0, starting transfers between devices: 14.4 us -> none  [the longest x6 14.1 us: passed_along(): lax.ppermute(array, axis, [(i, (i + by) % size) for i in range(size)])]
    dot_general x11 -> x0, matrix products: 3.74 us -> none  [fdot(): lax.dot_general(a, b, dims, precision=HIGH, preferred_element_type=F32)]
    all_gather x1 -> x0, blocking collectives: 1.92 us -> none  [shards(): bound = lax.all_gather(boundary_mass[0], 'grp', axis=0, tiled=True)]
    unnamed x20 -> x17, local copies, waits for them, and re-layouts: 6.32 us -> 7.75 us
  transfers between devices with their start and end apart: 13 -> 0, of which waited for: 11 -> 0; matrix products, arithmetic and copies ran while one was open for 1% -> 0% of each run, Pallas kernels for 9% -> 0%
where the time goes in v2:
time: 89.5 us; the launch traced here: 89.1 us
  Pallas kernels  80.7 us (90%)
  local copies, waits for them, and re-layouts  7.75 us (9%)
    pallas_call x1, Pallas kernels, interface(): pl.pallas_call(interface_kernel, out_shape=[block, block, jax.ShapeDtypeS...  61.8 us
    pallas_call x1, Pallas kernels, substructure(): pl.pallas_call(substructure_kernel, out_shape=[block, jax.ShapeDtypeStruc...  18.9 us
    unnamed x17, local copies, waits for them, and re-layouts  7.75 us

profile of v2, /device:TPU:0, one launch (start us, length us, event | category | flops | bytes accessed | tf_op | source)
XLA Modules:
  0.0 89.1 jit_solution(4670232400209317076)
XLA Ops:
  0.6 0.0 copy-start
  0.6 1.6 %copy-done = bf16[1,1024,1024]{2,1,0:T(8,128)(2,1)S(1)} copy-done((bf16[1,1024,1024]{2,1,0:T(8,128)(2,1)S(1)}, bf16[1,1024,1024]{2,1,0:T(8,128)(2,1)}, u32[]{:S(2)}) %copy-start) | copy-done | bytes 2097176
  2.2 0.0 copy-start.1
  2.2 1.0 %copy-done.1 = bf16[1,256,1024]{2,1,0:T(8,128)(2,1)S(1)} copy-done((bf16[1,256,1024]{2,1,0:T(8,128)(2,1)S(1)}, bf16[1,256,1024]{2,1,0:T(8,128)(2,1)}, u32[]{:S(2)}) %copy-start.1) | copy-done | bytes 524312
  3.3 0.0 copy-start.2
  3.3 1.0 %copy-done.2 = f32[1,256,512]{2,1,0:T(8,128)S(1)} copy-done((f32[1,256,512]{2,1,0:T(8,128)S(1)}, f32[1,256,512]{2,1,0:T(8,128)}, u32[]{:S(2)}) %copy-start.2) | copy-done | bytes 524312
  4.3 0.0 copy-start.4
  4.3 0.7 copy-done.4
  5.0 0.0 copy-start.5
  5.0 0.7 copy-done.5
  5.7 0.0 copy-start.6
  5.7 0.7 copy-done.6
  6.4 0.0 copy-start.3
  6.4 18.9 %substructure.1 = (f32[256,256]{1,0:T(8,128)S(1)}, f32[2,256,256]{2,1,0:T(8,128)S(1)}, f32[256,256]{1,0:T(8,128)S(1)}, f32[256,256]{1,0:T(8,128)S(1)}) custom-call(bf16[1024,1024]{1,0:T(8,128)(2,1)S(1)} %bitcast.7, bf16[256,1024]{1,0:T(8,128)(2,1)S(1)} %bitcast.8, f32[256,512]{1,0:T(8,128)S(1)} %bitcast.9, f32[1,1024]{1,0:T(1,128)S(1)} %copy-done.4, ...), custom_call_target="tpu_custom_call" | custom-call | tf_op jit(solution)/shard_map/substructure/pallas_call | solution.py:178
  25.3 0.0 copy-done.3
  25.3 61.8 %interface.1 = (f32[256,256]{1,0:T(8,128)S(1)}, f32[256,256]{1,0:T(8,128)S(1)}, f32[64,256]{1,0:T(8,128)S(1)}) custom-call(f32[256,256]{1,0:T(8,128)S(1)} %get-tuple-element.10.own_ref, f32[2,256,256]{2,1,0:T(8,128)S(1)} %get-tuple-element.11.move_ref, f32[256,256]{1,0:T(8,128)S(1)} %get-tuple-element.12.om_ref, f32[256,256]{1,0:T(8,128)S(1)} %get-tuple-element.13.mm_ref, ...), custom_call_target="tpu_custom_call" | custom-call | tf_op jit(solution)/shard_map/interface/pallas_call | solution.py:396
  87.1 0.7 copy.13
  87.8 0.7 copy.14
  88.5 0.6 copy.15
Async XLA Ops:
  0.6 1.6 %copy-start = (bf16[1,1024,1024]{2,1,0:T(8,128)(2,1)S(1)}, bf16[1,1024,1024]{2,1,0:T(8,128)(2,1)}, u32[]{:S(2)}) copy-start(bf16[1,1024,1024]{2,1,0:T(8,128)(2,1)} %param.7) | copy-start | bytes 6291460
  2.2 1.0 %copy-start.1 = (bf16[1,256,1024]{2,1,0:T(8,128)(2,1)S(1)}, bf16[1,256,1024]{2,1,0:T(8,128)(2,1)}, u32[]{:S(2)}) copy-start(bf16[1,256,1024]{2,1,0:T(8,128)(2,1)} %param.8) | copy-start | bytes 1572868
  3.3 1.0 %copy-start.2 = (f32[1,256,512]{2,1,0:T(8,128)S(1)}, f32[1,256,512]{2,1,0:T(8,128)}, u32[]{:S(2)}) copy-start(f32[1,256,512]{2,1,0:T(8,128)} %param.9) | copy-start | bytes 1572868
  4.3 0.7 copy-start.4
  5.0 0.7 copy-start.5
  5.7 0.7 copy-start.6
  6.4 18.9 %copy-start.3 = (f32[1,64,256]{2,1,0:T(8,128)S(1)}, f32[1,64,256]{2,1,0:T(8,128)}, u32[]{:S(2)}) copy-start(f32[1,64,256]{2,1,0:T(8,128)} %param.13) | copy-start | bytes 196612

commit v3 on v2

v3 whole, which is shorter than its diff:
```python
import functools
import jax
import jax.numpy as jnp
from jax import lax
from jax.experimental import pallas as pl
from jax.experimental.pallas import tpu as pltpu
from jax.sharding import PartitionSpec as P

F32 = jnp.float32
BF16 = jnp.bfloat16
HIGH = lax.Precision.HIGHEST
SMALL = 128
TILE = 256
VMEM_LIMIT = 56 * 2**20
NT = (((1,), (1,)), ((), ()))
NN = (((1,), (0,)), ((), ()))
TN = (((0,), (0,)), ((), ()))


def dot(a, b, dims=NN):
    return lax.dot_general(a, b, dims, preferred_element_type=F32)


def fdot(a, b, dims=NN):
    return lax.dot_general(a, b, dims, precision=HIGH, preferred_element_type=F32)


def split(x):
    hi = x.astype(BF16)
    return hi, (x - hi.astype(F32)).astype(BF16)


def dot3(a, b, dims=NN):
    ah, al = split(a)
    bh, bl = split(b)
    return dot(ah, bh, dims) + (dot(ah, bl, dims) + dot(al, bh, dims))


def iota(shape, dim):
    return lax.broadcasted_iota(jnp.int32, shape, dim)


def invert_diagonal(l_ref, inv, small):
    count = l_ref.shape[0] // SMALL
    rows = iota((SMALL, SMALL), 0)
    cols = iota((SMALL, SMALL), 1)

    def block(j):
        return l_ref[j * SMALL : (j + 1) * SMALL, j * SMALL : (j + 1) * SMALL]

    pair = ((rows >> 1) == (cols >> 1)) & (rows > cols)
    for j in range(count):
        full = block(j).astype(F32)
        diag = jnp.where(rows == cols, full, 0.0)
        down = 1.0 / jnp.sum(diag, axis=1, keepdims=True)
        across = 1.0 / jnp.sum(diag, axis=0, keepdims=True)
        first = jnp.where(rows == cols, down, 0.0)
        small[j] = first - jnp.where(pair, down * full * across, 0.0)

    def level(lev, carry):
        same = (rows >> (lev + 1)) == (cols >> (lev + 1))
        low = ((rows >> lev) & 1) > ((cols >> lev) & 1)
        mask = same & low
        for j in range(count):
            x = small[j]
            off = jnp.where(mask, block(j).astype(F32), 0.0).astype(BF16)
            xh, xl = split(x)
            mid = dot(jnp.concatenate([xh, xl], 1), jnp.concatenate([off, off], 0))
            mh, ml = split(mid)
            wide = dot(jnp.concatenate([mh, ml], 1), jnp.concatenate([xh, xh], 0))
            small[j] = x - (wide + dot(mh, xl))
        return carry

    lax.fori_loop(1, SMALL.bit_length() - 1, level, 0)
    for j in range(count // 2):
        upper, lower = small[2 * j], small[2 * j + 1]
        off = l_ref[(2 * j + 1) * SMALL : (2 * j + 2) * SMALL, 2 * j * SMALL : (2 * j + 1) * SMALL]
        lh, ll = split(lower)
        mid = dot(jnp.concatenate([lh, ll], 1), jnp.concatenate([off, off], 0))
        inv[j, :SMALL, :SMALL] = upper
        inv[j, :SMALL, SMALL:] = jnp.zeros((SMALL, SMALL), F32)
        inv[j, SMALL:, :SMALL] = -dot3(mid, upper)
        inv[j, SMALL:, SMALL:] = lower


def solve_modes(l_ref, c_ref, inv, wh, wl):
    for j in range(l_ref.shape[0] // TILE):
        at = slice(j * TILE, (j + 1) * TILE)
        acc = c_ref[:, at].astype(F32)
        if j:
            before = slice(0, j * TILE)
            acc = acc - (
                dot(wh[:, before], l_ref[at, before], NT)
                + dot(wl[:, before], l_ref[at, before], NT)
            )
        wh[:, at], wl[:, at] = split(dot3(acc, inv[j], NT))


def solve_constraint(l_ref, inv, wh, wl):
    ni = l_ref.shape[0]
    for j in reversed(range(ni // TILE)):
        at = slice(j * TILE, (j + 1) * TILE)
        acc = wh[:, at].astype(F32) + wl[:, at].astype(F32)
        if (j + 1) * TILE < ni:
            after = slice((j + 1) * TILE, ni)
            acc = acc + (dot(wh[:, after], l_ref[after, at]) + dot(wl[:, after], l_ref[after, at]))
        wh[:, at], wl[:, at] = split(-dot3(acc, inv[j]))


def inverse_of(p):
    m = len(p)
    if m == 1:
        return [[1.0 / p[0][0]]]
    if m == 2:
        scale = 1.0 / (p[0][0] * p[1][1] - p[0][1] * p[0][1])
        side = -p[0][1] * scale
        return [[p[1][1] * scale, side], [side, p[0][0] * scale]]
    h = m // 2
    span = range(h)
    ai = inverse_of([row[:h] for row in p[:h]])
    b = [row[h:] for row in p[:h]]
    w = [[sum(ai[i][k] * b[k][j] for k in span) for j in span] for i in span]
    s = [[None] * h for _ in span]
    for i in span:
        for j in range(i, h):
            s[i][j] = s[j][i] = p[h + i][h + j] - sum(b[k][i] * w[k][j] for k in span)
    si = inverse_of(s)
    v = [[sum(w[i][k] * si[k][j] for k in span) for j in span] for i in span]
    top = [[None] * h for _ in span]
    for i in span:
        for j in range(i, h):
            top[i][j] = top[j][i] = ai[i][j] + sum(v[i][k] * w[j][k] for k in span)
    out = [top[i] + [-v[i][j] for j in span] for i in span]
    return out + [[-v[j][i] for j in span] + si[i] for i in span]


def sweep(a, size, pivots=8):
    width = a.shape[1]
    lane = iota(a.shape, 1)
    row_at = iota(a.shape, 0)
    first = lane < size
    local = jnp.where(first, lane, lane - size)
    local_row = local[:1]

    def lanes(rows, k):
        left = rows[:, k : k + 1]
        if width == size:
            return jnp.broadcast_to(left, rows.shape)
        return jnp.where(first[: rows.shape[0]], left, rows[:, size + k : size + k + 1])

    for k in range(0, size, pivots):
        span = range(pivots)
        cols = [lanes(a, k + i) for i in span]
        rows = [a[k + i : k + i + 1, :] for i in span]
        small = [[cols[j][k + i : k + i + 1] for j in span] for i in span]
        small = [[small[min(i, j)][max(i, j)] for j in span] for i in span]
        inv = inverse_of(small)
        fresh = []
        for i in span:
            row = sum(inv[i][j] * rows[j] for j in span)
            for j in span:
                row = jnp.where(local_row == k + j, inv[i][j], row)
            fresh.append(row)
        inside = (local // pivots) == (k // pivots)
        a = jnp.where(inside, 0.0, a)
        for i in span:
            a = a - cols[i] * fresh[i]
        for i in span:
            a = jnp.where(row_at == k + i, fresh[i], a)
    return a


def invert(ref, step):
    n = ref.shape[0]
    for p in range(n // step):
        at = slice(p * step, (p + 1) * step)
        pin = sweep(ref[at, at], step)
        panel = ref[at, :]
        col = ref[:, at]
        inside = (iota((step, n), 1) // step) == p
        row = jnp.where(inside, 0.0, dot3(pin, panel))
        left = (iota((n, step), 0) // step) == p
        colz = jnp.where(left, 0.0, col)
        ref[...] = ref[...] - dot3(colz, row)
        ref[:, at] = -dot3(colz, pin)
        ref[at, :] = row
        ref[at, at] = pin


STEP = 64


def stages_of(size):
    stages, stride = [], 1
    while stride < size:
        radix = 4 if stride * 4 <= size else 2
        stages.append((stride, radix))
        stride *= radix
    return stages


def at_device(sub, grp):
    return dict(device_id=(sub, grp), device_id_type=pl.DeviceIdType.MESH)


def reduction_kernel(
    l_hbm, c_hbm, rows_hbm, weights_hbm, bound_hbm, map_hbm, loads_hbm,
    red_ref, mass_ref, out_ref,
    l_ref, c_ref, weights_ref, bound, map_ref, loads_ref, stiff,
    inv, small, wh, wl, both, move, move_mass, came,
    work, z, sy, near, acc, got, total,
    local, send, recv, part_send, part_recv, fwd_send, fwd_recv,
    dir_send, dir_recv, sum_send, sum_recv, all_send, all_recv,
):
    grp, sub = lax.axis_index("grp"), lax.axis_index("sub")
    members, size = lax.axis_size("grp"), lax.axis_size("sub")
    ahead, back = lax.rem(sub + 1, size), lax.rem(sub + size - 1, size)
    others = [lax.rem(grp + d, members) for d in range(1, members)]
    width = c_ref.shape[0]
    half = map_ref.shape[1]
    n = loads_ref.shape[0]
    stages = stages_of(size)
    mine = pl.ds(pl.multiple_of(grp * width, width), width)
    share = half // members
    part = pl.ds(pl.multiple_of(grp * share, share), share)

    loads_in = []
    for i, (src, dst) in enumerate([
        (l_hbm, l_ref), (c_hbm, c_ref), (rows_hbm, stiff.at[mine]), (bound_hbm, bound.at[grp]),
        (weights_hbm, weights_ref), (map_hbm, map_ref), (loads_hbm, loads_ref),
    ]):
        copy = pltpu.make_async_copy(src, dst, local.at[i])
        copy.start()
        loads_in.append(copy)

    def partner(stride, radix, d):
        digit = lax.rem(lax.div(sub, stride), radix)
        return sub + (lax.rem(digit + d, radix) - digit) * stride

    barrier = pltpu.get_barrier_semaphore()
    greeted = 0
    for other in others:
        pl.semaphore_signal(barrier, inc=1, **at_device(sub, other))
        greeted += 1
    for to in [ahead, back] + [partner(t, r, d) for t, r in stages for d in range(1, r)]:
        pl.semaphore_signal(barrier, inc=1, **at_device(to, grp))
        greeted += 1

    def remote(src, dst, send, recv, to_sub, to_grp):
        copy = pltpu.make_async_remote_copy(
            src_ref=src, dst_ref=dst, send_sem=send, recv_sem=recv, **at_device(to_sub, to_grp)
        )
        copy.start()
        return copy

    def spread(item, ref):
        return [
            remote(ref, ref, send.at[item, d], recv.at[item, d], sub, other)
            for d, other in enumerate(others)
        ]

    def to_back(item, ref):
        return remote(ref.at[part], came.at[item, part], part_send.at[item], part_recv.at[item], back, grp)

    def forward(item):
        return [
            remote(
                came.at[item, part], came.at[item, part],
                fwd_send.at[item, d], fwd_recv.at[item, d], sub, other,
            )
            for d, other in enumerate(others)
        ]

    def finished(copies):
        for copy in copies:
            copy.wait()

    loads_in[0].wait()
    invert_diagonal(l_ref, inv, small)
    pl.semaphore_wait(barrier, greeted)
    finished(loads_in[1:])
    stiff_copies = spread(2, stiff.at[mine])
    bound_copies = spread(3, bound.at[grp])
    solve_modes(l_ref, c_ref, inv, wh, wl)
    both[0, mine, :] = wh[...]
    modes_copies = spread(0, both.at[0, mine])
    finished(stiff_copies + modes_copies)

    q = jnp.where(iota((half, half), 0) == map_ref[...], 1.0, 0.0).astype(F32)
    wo, ws = both[0, :half], both[0, half:]
    shared = stiff[half:, half:] - dot(ws, ws, NT)
    move[0] = fdot(fdot(q, shared), q, NT)
    stiff_move = to_back(0, move.at[0])
    cross = stiff[half:, :half] - dot(ws, wo, NT)
    move[1] = fdot(q, cross)
    cross_move = to_back(1, move.at[1])

    solve_constraint(l_ref, inv, wh, wl)
    both[1, mine, :] = wh[...]
    constraint_copies = spread(1, both.at[1, mine])
    red_ref[...] = stiff[:half, :half] - dot(wo, wo, NT)

    stiff_move.wait()
    forwards = forward(0)
    cross_move.wait()
    cross_forwards = forward(1)
    finished(forwards)
    red_ref[...] = red_ref[...] + came[0]
    work[...] = red_ref[...]
    invert(work, STEP)
    z[...] = fdot(loads_ref[...], work[...])

    def neighbours(v, use):
        return [
            remote(v, near.at[use, 0], dir_send.at[use, 0], dir_recv.at[use, 0], ahead, grp),
            remote(v, near.at[use, 1], dir_send.at[use, 1], dir_recv.at[use, 1], back, grp),
        ]

    def from_neighbours(use):
        return fdot(near[use, 0], move[1]) + fdot(near[use, 1], came[1], NT)

    copies = neighbours(z, 0)
    y = fdot(z[...], red_ref[...])
    rho = fdot(loads_ref[...], z[...], NT)
    finished(cross_forwards + bound_copies + constraint_copies)
    weights = weights_ref[...]
    eye = iota((half, half), 0) == iota((half, half), 1)
    pieces = jnp.concatenate([bound[i] for i in range(members)], axis=1)

    def mass_of(c, b):
        ch, cl = split(c.astype(F32) * weights)
        return dot(ch, c, NT) + dot(cl, c, NT) + jnp.where(eye, b, 0.0)

    mass_shared = mass_of(both[1, half:], pieces[:, half:])
    move_mass[...] = fdot(fdot(q, mass_shared), q, NT)
    finished(copies)
    y = y + from_neighbours(0)
    sy[...] = fdot(y, work[...])
    copies = neighbours(sy, 1)
    mass_move = to_back(2, move_mass)
    y2 = fdot(sy[...], red_ref[...])
    acc[0, :n, :n] = rho
    acc[0, :n, n:] = fdot(z[...], y, NT)
    acc[0, n:, :n] = fdot(y, sy[...], NT)
    mass_ref[...] = mass_of(both[1, :half], pieces[:, :half])
    finished(copies)
    y2 = y2 + from_neighbours(1)
    acc[0, n:, n:] = fdot(sy[...], y2, NT)

    rows = 2 * n // members
    chunk = pl.ds(pl.multiple_of(grp * rows, rows), rows)
    slot = 0
    for i, (stride, radix) in enumerate(stages):
        copies = [
            remote(
                acc.at[i, chunk], got.at[slot + d - 1],
                sum_send.at[slot + d - 1], sum_recv.at[slot + d - 1],
                partner(stride, radix, d), grp,
            )
            for d in range(1, radix)
        ]
        value = acc[i, chunk, :]
        for d, copy in enumerate(copies):
            copy.wait()
            value = value + got[slot + d]
        acc[i + 1, chunk, :] = value
        slot += radix - 1
    last = len(stages)
    total[chunk, :] = acc[last, chunk, :]
    copies = [
        remote(acc.at[last, chunk], total.at[chunk], all_send.at[d], all_recv.at[d], sub, other)
        for d, other in enumerate(others)
    ]
    mass_move.wait()
    mass_forwards = forward(2)
    finished(copies)

    rho, gamma = total[:n, :n], total[:n, n:]
    kappa, delta = total[n:, :n], total[n:, n:]
    both = sweep(jnp.concatenate([gamma, rho], axis=1), n)
    gamma_inv, rho_inv = both[:, :n], both[:, n:]
    c1 = fdot(gamma_inv, rho)
    cross = fdot(gamma, c1)
    rho_next = rho - cross - cross.T + fdot(c1, fdot(kappa, c1), TN)
    beta = fdot(rho_inv, rho_next)
    eye = jnp.where(iota((n, n), 0) == iota((n, n), 1), 1.0, 0.0)
    pb = eye + beta
    mixed = fdot(pb, fdot(kappa, c1), TN)
    gamma2 = fdot(pb, fdot(gamma, pb), TN) - mixed - mixed.T + fdot(c1, fdot(delta, c1), TN)
    c2 = fdot(sweep(gamma2, n), rho_next)
    out_ref[...] = fdot(c1 + fdot(pb, c2), z[...], TN) - fdot(fdot(c1, c2), sy[...], TN)
    finished(mass_forwards)
    mass_ref[...] = mass_ref[...] + came[2]


def shards(
    interior_factor, coupling, boundary_stiffness, interior_mass, boundary_mass, dof_map, load_cases
):
    width, ni = coupling.shape[1:]
    nbound = boundary_stiffness.shape[2]
    half = nbound // 2
    n = load_cases.shape[1]
    size, members = lax.axis_size("sub"), lax.axis_size("grp")
    block = jax.ShapeDtypeStruct((half, half), F32)
    stages = stages_of(size)
    slots = sum(r - 1 for _, r in stages)
    peers = max(members - 1, 1)
    dma = pltpu.SemaphoreType.DMA
    outs = pl.pallas_call(
        reduction_kernel,
        out_shape=[block, block, jax.ShapeDtypeStruct((n, half), F32)],
        in_specs=[pl.BlockSpec(memory_space=pltpu.HBM)] * 7,
        out_specs=[pl.BlockSpec(memory_space=pltpu.VMEM)] * 3,
        scratch_shapes=[
            pltpu.VMEM((ni, ni), BF16),
            pltpu.VMEM((width, ni), BF16),
            pltpu.VMEM((1, ni), F32),
            pltpu.VMEM((members, 1, width), F32),
            pltpu.VMEM((1, half), jnp.int32),
            pltpu.VMEM((n, half), F32),
            pltpu.VMEM((nbound, nbound), F32),
            pltpu.VMEM((ni // TILE, TILE, TILE), F32),
            pltpu.VMEM((ni // SMALL, SMALL, SMALL), F32),
            pltpu.VMEM((width, ni), BF16),
            pltpu.VMEM((width, ni), BF16),
            pltpu.VMEM((2, nbound, ni), BF16),
            pltpu.VMEM((2, half, half), F32),
            pltpu.VMEM((half, half), F32),
            pltpu.VMEM((3, half, half), F32),
            pltpu.VMEM((half, half), F32),
            pltpu.VMEM((n, half), F32),
            pltpu.VMEM((n, half), F32),
            pltpu.VMEM((2, 2, n, half), F32),
            pltpu.VMEM((len(stages) + 1, 2 * n, 2 * n), F32),
            pltpu.VMEM((slots, 2 * n // members, 2 * n), F32),
            pltpu.VMEM((2 * n, 2 * n), F32),
            dma((7,)),
            dma((4, peers)), dma((4, peers)), dma((3,)), dma((3,)), dma((3, peers)), dma((3, peers)),
            dma((2, 2)), dma((2, 2)), dma((slots,)), dma((slots,)), dma((peers,)), dma((peers,)),
        ],
        compiler_params=pltpu.CompilerParams(
            vmem_limit_bytes=VMEM_LIMIT, collective_id=0, has_side_effects=True
        ),
        name="reduction",
    )(
        interior_factor[0], coupling[0], boundary_stiffness[0], interior_mass,
        boundary_mass, dof_map, load_cases[0],
    )
    return tuple(out[None] for out in outs)


def solution(mesh):
    return jax.shard_map(
        shards,
        mesh=mesh,
        in_specs=(
            P("sub", None, None),
            P("sub", "grp", None),
            P("sub", "grp", None),
            P("sub", None),
            P("sub", "grp"),
            P("sub", None),
            P("sub", None, None),
        ),
        out_specs=(P("sub", None, None), P("sub", None, None), P("sub", None, None)),
        check_vma=False,
    )
```

time: 89.5 us -> 75.2 us (0.84)
  Pallas kernels: 80.7 us -> 69.5 us
  local copies, waits for them, and re-layouts: 7.75 us -> 4.81 us
    pallas_call x2 -> x1, Pallas kernels: 80.7 us -> 69.5 us  [shards(): pl.pallas_call(reduction_kernel, out_shape=[block, block, jax.ShapeDtypeS...]
    unnamed x17 -> x3, local copies, waits for them, and re-layouts: 7.75 us -> 4.81 us
where the time goes in v3:
time: 75.2 us; the launch traced here: 75 us
  Pallas kernels  69.5 us (92%)
  local copies, waits for them, and re-layouts  4.81 us (6%)
    pallas_call x1, Pallas kernels, shards(): pl.pallas_call(reduction_kernel, out_shape=[block, block, jax.ShapeDtypeS...  69.5 us
    unnamed x3, local copies, waits for them, and re-layouts  4.81 us

profile of v3, /device:TPU:0, one launch (start us, length us, event | category | flops | bytes accessed | tf_op | source)
XLA Modules:
  0.0 75.0 jit_solution(10774500968373505336)
XLA Ops:
  0.6 69.5 %reduction.1 = (f32[256,256]{1,0:T(8,128)}, f32[256,256]{1,0:T(8,128)}, f32[64,256]{1,0:T(8,128)}) custom-call(bf16[1024,1024]{1,0:T(8,128)(2,1)} %bitcast.7, bf16[256,1024]{1,0:T(8,128)(2,1)} %bitcast.8, f32[256,512]{1,0:T(8,128)} %bitcast.9, f32[1,1024]{1,0:T(1,128)} %weights_hbm.1, f32[1,256]{1,0:T(1,128)} %bound_hbm.1, s32[1,256]{1,0:T(1,128)} %map_hbm.1, ...), custom_call_target="tpu_custom_call" | custom-call | tf_op jit(solution)/shard_map/reduction/pallas_call | solution.py:409
  70.2 1.7 %copy.13 = f32[1,256,256]{2,1,0:T(8,128)} copy(f32[1,256,256]{2,1,0:T(8,128)} %bitcast.11) | data formatting | bytes 524288
  71.8 1.7 %copy.14 = f32[1,256,256]{2,1,0:T(8,128)} copy(f32[1,256,256]{2,1,0:T(8,128)} %bitcast.10) | data formatting | bytes 524288
  73.5 1.5 %copy.15 = f32[1,64,256]{2,1,0:T(8,128)} copy(f32[1,64,256]{2,1,0:T(8,128)} %bitcast.13) | data formatting | bytes 131072

commit v4 on v3

--- a/solution.py
+++ b/solution.py
@@ -391,6 +391,27 @@
     out_ref[...] = fdot(c1 + fdot(pb, c2), z[...], TN) - fdot(fdot(c1, c2), sy[...], TN)
     finished(mass_forwards)
     mass_ref[...] = mass_ref[...] + came[2]
+
+
+def written_kernel(*refs):
+    count = len(refs) // 2
+    sems = refs[-1]
+    copies = [pltpu.make_async_copy(refs[i], refs[count + i], sems.at[i]) for i in range(count)]
+    for copy in copies:
+        copy.start()
+    for copy in copies:
+        copy.wait()
+
+
+def written(arrays):
+    return pl.pallas_call(
+        written_kernel,
+        out_shape=[jax.ShapeDtypeStruct(a.shape, a.dtype) for a in arrays],
+        in_specs=[pl.BlockSpec(memory_space=pltpu.HBM)] * len(arrays),
+        out_specs=[pl.BlockSpec(memory_space=pltpu.HBM)] * len(arrays),
+        scratch_shapes=[pltpu.SemaphoreType.DMA((len(arrays),))],
+        name="written",
+    )(*arrays)
 
 
 def shards(
@@ -446,7 +467,7 @@
         interior_factor[0], coupling[0], boundary_stiffness[0], interior_mass,
         boundary_mass, dof_map, load_cases[0],
     )
-    return tuple(out[None] for out in outs)
+    return tuple(out[None] for out in written(outs))
 
 
 def solution(mesh):

time: 75.2 us -> 89.5 us (1.19)
  Pallas kernels: 69.5 us -> 88.5 us
  local copies, waits for them, and re-layouts: 4.81 us -> 0 us
    pallas_call x0 -> x1, Pallas kernels: none -> 19 us  [written(): pl.pallas_call(written_kernel, out_shape=[jax.ShapeDtypeStruct(a.shape, a...]
    unnamed x3 -> x0, local copies, waits for them, and re-layouts: 4.81 us -> none
where the time goes in v4:
time: 89.5 us; the launch traced here: 89.3 us
  Pallas kernels  88.5 us (99%)
    pallas_call x1, Pallas kernels, shards(): pl.pallas_call(reduction_kernel, out_shape=[block, block, jax.ShapeDtypeS...  69.5 us
    pallas_call x1, Pallas kernels, written(): pl.pallas_call(written_kernel, out_shape=[jax.ShapeDtypeStruct(a.shape, a...  19 us

profile of v4, /device:TPU:0, one launch (start us, length us, event | category | flops | bytes accessed | tf_op | source)
XLA Modules:
  0.0 89.3 jit_solution(3520098855957073257)
XLA Ops:
  0.6 69.5 %reduction.1 = (f32[256,256]{1,0:T(8,128)}, f32[256,256]{1,0:T(8,128)}, f32[64,256]{1,0:T(8,128)}) custom-call(bf16[1024,1024]{1,0:T(8,128)(2,1)} %bitcast.7, bf16[256,1024]{1,0:T(8,128)(2,1)} %bitcast.8, f32[256,512]{1,0:T(8,128)} %bitcast.9, f32[1,1024]{1,0:T(1,128)} %weights_hbm.1, f32[1,256]{1,0:T(1,128)} %bound_hbm.1, s32[1,256]{1,0:T(1,128)} %map_hbm.1, ...), custom_call_target="tpu_custom_call" | custom-call | tf_op jit(solution)/shard_map/reduction/pallas_call | solution.py:430
  70.2 19.0 %written.1 = (f32[256,256]{1,0:T(8,128)}, f32[256,256]{1,0:T(8,128)}, f32[64,256]{1,0:T(8,128)}) custom-call(f32[256,256]{1,0:T(8,128)} %get-tuple-element.9.refs_0_, f32[256,256]{1,0:T(8,128)} %get-tuple-element.10.refs_1_, f32[64,256]{1,0:T(8,128)} %get-tuple-element.11.refs_2_), custom_call_target="tpu_custom_call" | custom-call | tf_op jit(solution)/shard_map/written/pallas_call | solution.py:407
